TPU v7x, 128 devices: a whole 4x4x4 slice. The times are simulated.
128 devices in a mesh: expert: 8 (over x, core), shard: 16 (over z, y).
Axes of the slice: x: 4, y: 4, z: 4, core: 2. Of those that a mesh axis runs over, the one named last changes fastest.
Arguments:
- tokens_in: bfloat16 [4096, 4096], P(('expert', 'shard')), may hold values from -6 to 6
- out_grad: bfloat16 [4096, 2, 8192], P(('expert', 'shard')), may hold values from -6 to 6
- expert_ids: int32 [4096, 2], P(('expert', 'shard')), may hold values from 0 to 7, all different within a row; in each aligned block of 32 rows (0 to 31, 32 to 63, ...) at most 10 rows name the same one
- d_levels: int32 [8, 16], P('expert'), may hold values from 0 to 7
- f_levels: int32 [8, 32], P('expert', 'shard'), may hold values from 0 to 7
Outputs:
- ascent: bfloat16 [8, 4096, 8192], P('expert', None, 'shard')
Inputs may be any that keep to these rules, and one draw needn't show every extreme that they name: `expert_ids`: each token names two different experts; among the 64 entries of one device no expert is named more than 10 times, and 10 is reached on some device; every expert is named somewhere.
All inputs are finite; a program needn't handle non-finite values.
Results may differ from a plain program's by a relative error of at most 0.001.
Values may be sent and summed in bfloat16 or wider, within the bound.
No kernel may reach another device: no remote copies, remote signals or barrier semaphores. Data moves between devices by JAX's collectives and lax.ppermute only.
A program may use at most 128 MiB of HBM per device.

v0:
```python
import jax
import jax.numpy as jnp
from jax import lax
from jax.sharding import PartitionSpec as P

BLK = 256


def invert_blocks(blocks):
    lower = jnp.linalg.cholesky(blocks)
    identity = jnp.eye(blocks.shape[-1], dtype=blocks.dtype)
    return jax.vmap(lambda factor: jax.scipy.linalg.cho_solve((factor, True), identity))(lower)


def damping(levels):
    return 0.05 * jnp.exp(0.4 * levels.astype(jnp.float32))


def covariance(rows, levels, row_count):
    blocks = rows.reshape(rows.shape[0], -1, BLK)
    cov = jnp.einsum("rbi,rbj->bij", blocks, blocks, preferred_element_type=jnp.float32) / row_count
    return cov + damping(levels)[:, None, None] * jnp.eye(BLK, dtype=jnp.float32)


def local(tokens_in, out_grad, expert_ids, d_levels, f_levels):
    group_count = lax.axis_size("expert")
    shard_count = lax.axis_size("shard")
    tok_rows = tokens_in.shape[0]
    width = tokens_in.shape[1]
    ff_full = out_grad.shape[2]
    ff_dev = ff_full // shard_count
    capacity = min(tok_rows, max(2, 5 * tok_rows // (2 * group_count)))
    slot_total = group_count * capacity
    flat_ids = expert_ids.reshape(-1)
    member = (flat_ids[:, None] == jnp.arange(group_count, dtype=jnp.int32)[None, :]).astype(
        jnp.int32
    )
    before = jnp.cumsum(member, axis=0) - member
    ranking = jnp.sum(before * member, axis=1)
    target = flat_ids * capacity + ranking
    dispatch = (jnp.arange(slot_total, dtype=jnp.int32)[:, None] == target[None, :]).astype(
        jnp.bfloat16
    )
    per_token = jnp.sum(
        dispatch.reshape(slot_total, tok_rows, 2).astype(jnp.float32), axis=2
    ).astype(jnp.bfloat16)
    x_send = jnp.dot(per_token, tokens_in, preferred_element_type=jnp.float32).astype(jnp.bfloat16)
    g_send = jnp.dot(
        dispatch, out_grad.reshape(2 * tok_rows, ff_full), preferred_element_type=jnp.float32
    ).astype(jnp.bfloat16)
    valid_slot = jnp.sum(dispatch.astype(jnp.float32), axis=1).astype(jnp.bfloat16)
    x_group, g_group, v_group = (
        lax.all_to_all(
            x_send.reshape(group_count, capacity, width),
            "expert",
            split_axis=0,
            concat_axis=1,
            tiled=True,
        ),
        lax.all_to_all(
            g_send.reshape(group_count, capacity, ff_full),
            "expert",
            split_axis=0,
            concat_axis=1,
            tiled=True,
        ),
        lax.all_to_all(
            valid_slot.reshape(group_count, capacity),
            "expert",
            split_axis=0,
            concat_axis=1,
            tiled=True,
        ),
    )
    rows_x, live_rows = (
        lax.all_gather(x_group, "shard", axis=1, tiled=True),
        lax.all_gather(v_group, "shard", axis=1, tiled=True),
    )
    rows_g = lax.all_to_all(g_group, "shard", split_axis=2, concat_axis=1, tiled=True)
    rows_x = rows_x.reshape(-1, width)
    rows_g = rows_g.reshape(-1, ff_dev)
    row_count = jnp.sum(live_rows.astype(jnp.float32))
    gradient = lax.dot_general(
        rows_x, rows_g, (((0,), (0,)), ((), ())), preferred_element_type=jnp.float32
    )
    inv_f = invert_blocks(covariance(rows_g, f_levels[0], row_count))
    grad_blocks = gradient.reshape(width // BLK, BLK, ff_dev)
    highest = lax.Precision.HIGHEST
    own_blocks = width // BLK // shard_count
    first_block = lax.axis_index("shard") * own_blocks
    own_rows = lax.dynamic_slice_in_dim(rows_x, first_block * BLK, own_blocks * BLK, 1)
    own_levels = lax.dynamic_slice_in_dim(d_levels[0], first_block, own_blocks, 0)
    inv_a = invert_blocks(covariance(own_rows, own_levels, row_count))
    left_done = jnp.einsum(
        "bij,bjf->bif",
        lax.all_gather(inv_a, "shard", axis=0, tiled=True),
        grad_blocks,
        precision=highest,
    )
    precond = jnp.einsum(
        "dcj,cjk->dck", left_done.reshape(width, ff_dev // BLK, BLK), inv_f, precision=highest
    ).reshape(width, ff_dev)
    norm_total = lax.psum(jnp.sum(precond * precond), ("expert", "shard"))
    ascent_scale = lax.rsqrt(norm_total / (group_count * width * ff_full) + 1e-06)
    return (precond * ascent_scale).astype(jnp.bfloat16)[None]


def solution(mesh):
    return jax.shard_map(
        local,
        mesh=mesh,
        in_specs=(
            P(("expert", "shard"), None),
            P(("expert", "shard"), None, None),
            P(("expert", "shard"), None),
            P("expert", None),
            P("expert", "shard"),
        ),
        out_specs=P("expert", None, "shard"),
        check_vma=False,
    )
```

profile of v0, /device:TPU:1, one launch (start us, length us, event | category | flops | bytes accessed | tf_op | source)
XLA Modules:
  0.0 557.9 jit_solution(17110452250015849158)
XLA Ops:
  9.4 20.7 %all_to_all.56 = bf16[8,10,4096]{2,1,0:T(8,128)(2,1)S(1)} all-to-all(bf16[8,10,4096]{2,1,0:T(8,128)(2,1)S(1)} %reshape.294), channel_id=1, replica_groups=mesh['expert'=8,'shard'=16] {'expert'}, dimensions={0} | all-to-all | bytes 1310720 | tf_op jit(solution)/shard_map/all_to_all | solution.py:53
  31.9 4.2 all-to-all-start.2
  42.4 4.8 all-to-all-start
  47.6 35.3 %all-reduce.2 = bf16[1280]{0:T(1024)(128)(2,1)S(1)} all-reduce(bf16[1280]{0:T(1024)(128)(2,1)S(1)} %dynamic-update-slice.22), channel_id=1, replica_groups=mesh['expert'=8,'shard'=16] {'shard'}, use_global_device_ids=true, to_apply=%add.2 | all-reduce | flops 1280 | bytes 5120
  83.6 29.6 %all-gather.3.cloned.1.call-done = bf16[1,1280,4096]{2,1,0:T(8,128)(2,1)} async-done(((bf16[1,80,4096]{2,1,0:T(8,128)(2,1)}), bf16[1,1280,4096]{2,1,0:T(8,128)(2,1)}) %all-gather.3.cloned.1.call-update) | async-done | bytes 10485776 | tf_op jit(solution)/shard_map/all_gather | solution.py:76
  113.2 2.5 fusion.7
  115.9 11.7 %custom-call.44 = f32[1,128,128]{2,1,0:T(8,128)S(1)} custom-call(f32[1,128,128]{2,1,0:T(8,128)S(1)} %cholesky.242), custom_call_target="Cholesky" | custom-call | tf_op jit(solution)/shard_map/jit(cholesky)/cholesky | solution.py:10
  127.7 9.8 %custom-call.45 = f32[1,1,128,128]{2,3,1,0:T(8,128)S(1)} custom-call(f32[1,1,128,128]{3,2,1,0:T(8,128)S(1)} %get-tuple-element.49), custom_call_target="InvertDiagBlocksLowerTriangular" | custom-call | tf_op jit(solution)/shard_map/jit(cholesky)/cholesky | solution.py:10
  138.0 11.7 %custom-call.46 = f32[1,128,128]{2,1,0:T(8,128)S(1)} custom-call(f32[1,128,128]{2,1,0:T(8,128)S(1)} %fusion.10), custom_call_target="Cholesky" | custom-call | tf_op jit(solution)/shard_map/jit(cholesky)/cholesky | solution.py:10
  151.7 4.0 while.3
  156.3 19.7 %custom-call.47 = f32[1,2,128,128]{2,3,1,0:T(8,128)S(1)} custom-call(f32[1,2,128,128]{3,2,1,0:T(8,128)S(1)} %bitcast.154), custom_call_target="InvertDiagBlocksLowerTriangular" | custom-call | tf_op jit(solution)/shard_map/vmap(jit(_cho_solve))/triangular_solve | solution.py:12
  179.8 9.3 %copy.119 = bf16[1,80,8192]{1,0,2:T(2,128)(2,1)} copy(bf16[1,80,8192]{2,1,0:T(8,128)(2,1)} %all_to_all.42) | data formatting | bytes 2621440 | tf_op jit(solution)/shard_map/all_to_all | solution.py:60
  189.7 45.2 %reduce.36 = bf16[8192,80]{1,0:T(8,128)(2,1)S(1)} reduce(bf16[8192,1,80]{2,1,0:T(2,128)(2,1)} %bitcast.142, bf16[]{:T(256)} %broadcast.338), dimensions={1}, to_apply=%bitcast.100.reduce_sub_computation | reduce | bytes 2621442
  235.0 4.6 reshape.358
  239.6 4.9 all-to-all-start.1
  248.9 14.6 %all-to-all-done.1 = bf16[16,2,20480]{2,1,0:T(2,128)(2,1)S(1)} async-done(((bf16[16,2,20480]{2,1,0:T(2,128)(2,1)}), bf16[16,2,20480]{2,1,0:T(2,128)(2,1)S(1)}, u32[]{:S(2)}, u32[]{:S(2)}) %all-to-all-start.1) | async-done | bytes 1310752 | tf_op jit(solution)/shard_map/all_to_all | solution.py:79
  263.5 8.1 %reshape.359 = bf16[8192,1,80]{2,1,0:T(2,128)(2,1)} reshape(bf16[16,2,20480]{2,1,0:T(2,128)(2,1)S(1)} %all-to-all-done.1) | data formatting | bytes 2621440
  271.6 8.2 %copy.120 = bf16[1,80,8192]{2,1,0:T(8,128)(2,1)S(1)} copy(bf16[1,80,8192]{1,0,2:T(2,128)(2,1)} %bitcast.144) | data formatting | bytes 2621440 | tf_op jit(solution)/shard_map/all_to_all | solution.py:79
  284.2 23.5 %custom-call.40 = f32[2,128,128]{2,1,0:T(8,128)S(1)} custom-call(f32[2,128,128]{2,1,0:T(8,128)S(1)} %cholesky.239), custom_call_target="Cholesky" | custom-call | tf_op jit(solution)/shard_map/jit(cholesky)/cholesky | solution.py:10
  308.4 19.7 %custom-call.41 = f32[2,1,128,128]{2,3,1,0:T(8,128)S(1)} custom-call(f32[2,1,128,128]{3,2,1,0:T(8,128)S(1)} %select_bitcast_fusion), custom_call_target="InvertDiagBlocksLowerTriangular" | custom-call | tf_op jit(solution)/shard_map/jit(cholesky)/cholesky | solution.py:10
  328.8 23.6 %custom-call.42 = f32[2,128,128]{2,1,0:T(8,128)S(1)} custom-call(f32[2,128,128]{2,1,0:T(8,128)S(1)} %convolution_subtract_fusion.3), custom_call_target="Cholesky" | custom-call | tf_op jit(solution)/shard_map/jit(cholesky)/cholesky | solution.py:10
  352.8 5.4 while.2
  353.4 2.1 bitcast_dynamic-update-slice_fusion.5
  358.2 40.1 %custom-call.43 = f32[2,2,128,128]{2,3,1,0:T(8,128)S(1)} custom-call(f32[2,2,128,128]{3,2,1,0:T(8,128)} %bitcast.153), custom_call_target="InvertDiagBlocksLowerTriangular" | custom-call | tf_op jit(solution)/shard_map/vmap(jit(_cho_solve))/triangular_solve | solution.py:12
  400.7 14.4 %copy.138 = bf16[4096,1280]{1,0:T(8,128)(2,1)} copy(bf16[4096,1280]{0,1:T(8,128)(2,1)} %bitcast.145) | data formatting | bytes 20971520 | tf_op jit(solution)/shard_map/dot_general | solution.py:83
  415.2 11.9 %fusion.46 = f32[16,256,512]{2,1,0:T(8,128)} fusion(bf16[16,256,1280]{2,1,0:T(8,128)(2,1)} %bitcast.146, bf16[1280,512,1]{1,0,2:T(8,128)(2,1)S(1)} %bitcast.147), kind=kOutput, calls=%fused_computation.106 | convolution fusion | flops 5368709120 | bytes 20185088 | tf_op jit(solution)/shard_map/dot_general | solution.py:83
  427.0 16.5 %fusion.47 = f32[16,256,512]{2,1,0:T(8,128)} fusion(f32[16,256,256]{2,1,0:T(8,128)} %all-gather.5.cloned.1.call-done, f32[16,256,512]{2,1,0:T(8,128)} %fusion.46), kind=kOutput, calls=%fused_computation.107 | convolution fusion | flops 6442450944 | bytes 20971520 | tf_op jit(solution)/shard_map/bij,bjf->bif/dot_general | solution.py:94
  443.5 10.5 %reshape.305 = f32[4096,2,256]{2,1,0:T(2,128)} reshape(f32[16,256,512]{2,1,0:T(8,128)} %fusion.47) | data formatting | bytes 16777216 | tf_op jit(solution)/shard_map/reshape | solution.py:101
  454.0 18.4 %multiply_reduce_fusion = (f32[]{:T(128)}, f32[2,256,4096]{2,1,0:T(8,128)}) fusion(f32[4096,2,256]{2,1,0:T(2,128)} %reshape.305, f32[2,128,256]{2,1,0:T(8,128)S(1)} %fusion.26, f32[2,128,256]{2,1,0:T(8,128)S(1)} %fusion.25), kind=kOutput, calls=%fused_computation.8 | convolution fusion | flops 6446776320 | bytes 17301508 | tf_op jit(solution)/shard_map/dcj,cjk->dck/dot_general | solution.py:100
  472.4 65.0 %psum.7 = f32[]{:T(128)} all-reduce(f32[]{:T(128)} %get-tuple-element.54), channel_id=1, replica_groups=mesh['expert'=8,'shard'=16] {'expert','shard'}, use_global_device_ids=true, to_apply=%region_14.15 | all-reduce | flops 1 | bytes 8 | tf_op jit(solution)/shard_map/psum | solution.py:103
  538.2 6.3 %multiply_convert_fusion = bf16[2,256,4096]{2,1,0:T(8,128)(2,1)} fusion(f32[2,256,4096]{2,1,0:T(8,128)} %get-tuple-element.55, f32[]{:T(128)S(6)} %rsqrt.3), kind=kLoop, calls=%fused_computation.7 | loop fusion | flops 4194304 | bytes 12582916 | tf_op jit(solution)/shard_map/convert_element_type | solution.py:105
  544.4 6.4 %copy.142 = bf16[1,4096,512]{2,1,0:T(8,128)(2,1)} copy(bf16[1,4096,512]{1,2,0:T(8,128)(2,1)} %bitcast.143) | data formatting | bytes 8388608 | tf_op jit(solution)/shard_map/convert_element_type | solution.py:105
  (119 shorter events, 36.8 us)
Async XLA Ops:
  6.5 2.2 copy-start
  6.5 29.6 %copy-start.5 = (s32[1,16]{1,0:T(1,128)S(1)}, s32[1,16]{1,0:T(1,128)}, u32[]{:S(2)}) copy-start(s32[1,16]{1,0:T(1,128)} %param.8) | copy-start | bytes 196
  6.5 106.6 %all-gather.3.cloned.1.call-start = ((), (), s32[]{:S(2)}) async-start(), calls=%async_computation.4 | async-start | bytes 11141120 | tf_op jit(solution)/shard_map/all_gather | solution.py:76
  31.1 10.0 %copy-start.9 = (u32[128]{0:T(128)S(1)}, u32[128]{0:T(128)}, u32[]{:S(2)}) copy-start(u32[128]{0:T(128)} %constant.269) | copy-start | bytes 1540
  31.9 10.5 %all-to-all-start.2 = ((bf16[8,1,10]{2,1,0:T(2,128)(2,1)}), bf16[8,1,10]{2,1,0:T(2,128)(2,1)S(1)}, u32[]{:S(2)}, u32[]{:S(2)}) async-start(bf16[8,1,10]{2,1,0:T(2,128)(2,1)} %all_to_all.51), calls=%async_computation.2 | async-start | bytes 8192 | tf_op jit(solution)/shard_map/all_to_all | solution.py:67
  42.4 136.0 %all-to-all-start = ((bf16[8,10,8192]{2,1,0:T(8,128)(2,1)}), bf16[8,10,8192]{2,1,0:T(8,128)(2,1)S(1)}, u32[]{:S(2)}, u32[]{:S(2)}) async-start(bf16[8,10,8192]{2,1,0:T(8,128)(2,1)} %reshape.293), calls=%async_computation | async-start | bytes 4194304 | tf_op jit(solution)/shard_map/all_to_all | solution.py:60
  47.3 379.8 %all-gather.5.cloned.1.call-start = ((), (), s32[]{:S(2)}) async-start(), calls=%async_computation.5 | async-start | bytes 4456448 | tf_op jit(solution)/shard_map/all_gather | solution.py:96
  155.7 0.6 copy-start.7
  235.0 13.3 %copy-start.6 = (s32[1,2]{1,0:T(1,128)S(1)}, s32[1,2]{1,0:T(1,128)}, u32[]{:S(2)}) copy-start(s32[1,2]{1,0:T(1,128)} %param.9) | copy-start | bytes 28
  239.6 23.8 %all-to-all-start.1 = ((bf16[16,2,20480]{2,1,0:T(2,128)(2,1)}), bf16[16,2,20480]{2,1,0:T(2,128)(2,1)S(1)}, u32[]{:S(2)}, u32[]{:S(2)}) async-start(bf16[16,2,20480]{2,1,0:T(2,128)(2,1)} %reshape.358), calls=%async_computation.1 | async-start | bytes 2621440 | tf_op jit(solution)/shard_map/all_to_all | solution.py:79
  281.1 1.9 copy-start.2
  282.7 69.9 %copy-start.4 = (pred[256,256]{1,0:T(8,128)(4,1)S(1)}, pred[256,256]{1,0:T(8,128)(4,1)}, u32[]{:S(2)}) copy-start(pred[256,256]{1,0:T(8,128)(4,1)} %iota_compare_fusion.4) | copy-start | bytes 196612
  282.8 70.0 %copy-start.8 = (s32[2,2]{1,0:T(2,128)S(1)}, s32[2,2]{1,0:T(2,128)}, u32[]{:S(2)}) copy-start(s32[2,2]{1,0:T(2,128)} %copy-done.7) | copy-start | bytes 52
  283.0 115.8 %copy-start.3 = (f32[128,256]{1,0:T(8,128)S(1)}, f32[128,256]{1,0:T(8,128)}, u32[]{:S(2)}) copy-start(f32[128,256]{1,0:T(8,128)} %copy.132) | copy-start | bytes 393220
  544.4 6.4 %copy-start.1 = (bf16[32,4096]{1,0:T(8,128)(2,1)S(1)}, bf16[32,4096]{1,0:T(8,128)(2,1)}, u32[]{:S(2)}) copy-start(bf16[32,4096]{1,0:T(8,128)(2,1)} %param.5) | copy-start | bytes 786436
Sparse Core Ops, SparseCore 0:
  31.3 81.8 all-gather.2
  178.6 50.7 all-gather.4
where the time goes:
time: 563 us; the launch traced here: 558 us
  other arithmetic  220 us (39%)
  blocking collectives  121 us (21%)
  local copies, waits for them, and re-layouts  84.3 us (15%)
  matrix products  56.6 us (10%)
  waiting for transfers between devices  44.2 us (8%)
  between operations  17.4 us (3%)
  starting transfers between devices  14 us (2%)
    another operation x15, other arithmetic, invert_blocks(): lower = jnp.linalg.cholesky(blocks)  102 us
    psum x1, blocking collectives, local(): norm_total = lax.psum(jnp.sum(precond * precond), ('expert', 'shard'))  65 us
    another operation x7, other arithmetic, invert_blocks(): jax.scipy.linalg.cho_solve((factor, True), identity)  61.3 us
    unnamed x3, other arithmetic  45.2 us
    unnamed x1, blocking collectives  35.3 us
    all_gather x1, waiting for transfers between devices, local(): lax.all_gather(x_group, 'shard', axis=1, tiled=True)  29.6 us
    all_to_all x1, blocking collectives, local(): lax.all_to_all(x_send.reshape(group_count, capacity, width), 'expert', sp...  20.7 us
    dot_general x1, matrix products, local(): jnp.einsum('dcj,cjk->dck', left_done.reshape(width, ff_dev // BLK, BLK),...  18.4 us
  transfers between devices with their start and end apart: 5, of which 2 were waited for; matrix products, arithmetic and copies ran while one was open for 53% of the time, Pallas kernels for 0%

commit v1 on v0

v1 whole, which is shorter than its diff:
```python
import functools

import jax
import jax.numpy as jnp
from jax import lax
from jax.experimental import pallas as pl
from jax.experimental.pallas import tpu as pltpu
from jax.sharding import PartitionSpec as P

BLK = 256
BASE = 32
PANEL = 8
F32 = jnp.float32
BF = jnp.bfloat16
TN = (((0,), (0,)), ((), ()))
VMEM = 56 << 20
PARAMS = pltpu.CompilerParams(vmem_limit_bytes=VMEM)


def iota(shape, dim):
    return lax.broadcasted_iota(jnp.int32, shape, dim)


def div(value, by):
    return (value * (65536 // by + 1)) >> 16


def onehot(hit):
    return jnp.where(hit, 1.0, 0.0).astype(BF)


def split2(x):
    high = x.astype(BF)
    return high, (x - high.astype(F32)).astype(BF)


def split3(x):
    high = x.astype(BF)
    rest = x - high.astype(F32)
    mid = rest.astype(BF)
    return high, mid, (rest - mid.astype(F32)).astype(BF)


def tn_full(a, b):
    ah, am, al = split3(a)
    bh, bm, bl = split3(b)
    return lax.dot_general(
        jnp.concatenate([ah, ah, am, ah, al, am], 0),
        jnp.concatenate([bh, bm, bh, bl, bh, bm], 0),
        TN,
        preferred_element_type=F32,
    )


def dot3(a, b):
    ah, al = a
    bh, bl = b
    dot = functools.partial(jnp.dot, preferred_element_type=F32)
    return dot(ah, bh) + (dot(ah, bl) + dot(al, bh))


def invert_base(packs):
    lane, sub = iota((BASE, 128), 1), iota((BASE, 128), 0)
    start = (lane // BASE) * BASE
    inner = lane - start
    packs = list(packs)
    for k0 in range(0, BASE, PANEL):
        cols = [
            [jnp.take_along_axis(x, start + (k0 + j), axis=1) for j in range(PANEL)] for x in packs
        ]
        for j in range(PANEL):
            k = k0 + j
            is_col, is_row = inner == k, sub == k
            for g, x in enumerate(packs):
                col = cols[g][j]
                inv = 1.0 / col[k : k + 1, :]
                row = jnp.where(is_col[:1], 1.0, x[k : k + 1, :]) * inv
                for jj in range(j + 1, PANEL):
                    other = cols[g][jj]
                    scaled = other[k : k + 1, :] * inv
                    cols[g][jj] = jnp.where(is_row, scaled, other - col * scaled)
                packs[g] = jnp.where(is_row, row, jnp.where(is_col, 0.0, x) - col * row)
    return packs


def invert_all(m_ref, count):
    per = 128 // BASE
    lane, sub = iota((BASE, BLK), 1), iota((BASE, BLK), 0)
    wide = iota((BLK, BLK), 1)
    for low in range(0, BLK, BASE):
        end = low + BASE
        packs = [
            jnp.concatenate(
                [m_ref[min(g + j, count - 1), low:end, low:end] for j in range(per)], axis=1
            )
            for g in range(0, count, per)
        ]
        packs = invert_base(packs)
        own = (lane >= low) & (lane < end)
        minus_eye = jnp.where(lane - low == sub, -1.0, 0.0)
        for m in range(count):
            at = (m % per) * BASE
            pivot = packs[m // per][:, at : at + BASE]
            rows = m_ref[m, low:end, :]
            new_rows = tn_full(pivot, jnp.where(own, minus_eye, rows))
            change = tn_full(jnp.where(own, 0.0, rows), new_rows)
            m_ref[m] = jnp.where((wide >= low) & (wide < end), 0.0, m_ref[m]) - change
            m_ref[m, low:end, :] = new_rows


def slots(id_col, id_row, first, step, capacity):
    shape = (id_col.shape[0], id_row.shape[1])
    earlier = iota(shape, 0) < first + step * iota(shape, 1)
    same = (id_col == id_row) & earlier
    rank = jnp.sum(jnp.where(same, 1, 0), axis=0, keepdims=True)
    return id_row, rank


def send_x_kernel(cap, parts, col_ref, first_ref, second_ref, x_ref, out_ref):
    rows, toks = out_ref.shape[0], x_ref.shape[0]
    width = x_ref.shape[1] // parts
    per = cap * parts
    hot = []
    for part in range(parts):
        total = None
        for j, ids in enumerate((first_ref, second_ref)):
            expert, rank = slots(col_ref[...], ids[...], j, 2, cap)
            target = expert * per + part * cap + rank
            hit = jnp.where(iota((rows, toks), 0) == target, 1.0, 0.0)
            total = hit if total is None else total + hit
        hot.append(total.astype(BF))
    data = jnp.concatenate([x_ref[:, p * width : (p + 1) * width] for p in range(parts)], 0)
    out_ref[...] = jnp.dot(
        jnp.concatenate(hot, 1), data, preferred_element_type=F32
    ).astype(BF)


def take_x_kernel(cap, parts, in_ref, out_ref):
    groups, per, width = in_ref.shape
    data = in_ref[...].reshape(groups * per, width)
    shape = (groups * cap, groups * per)
    row = iota(shape, 0)
    source = div(row, cap)
    base = source * per + (row - source * cap)
    for part in range(parts):
        pick = onehot(iota(shape, 1) == base + part * cap)
        out_ref[:, part * width : (part + 1) * width] = jnp.dot(
            pick, data, preferred_element_type=F32
        ).astype(BF)


def payload_kernel(cap, rows, nx, ng, col_ref, row_ref, first_ref, second_ref, x_ref, g_ref,
                   out_ref, hot_ref, add_ref):
    groups = out_ref.shape[1]
    toks, pairs = x_ref.shape[0], g_ref.shape[0]
    total = groups * rows

    @pl.when(pl.program_id(0) == 0)
    def _():
        for part in range(nx):
            hit = None
            for j, ids in enumerate((first_ref, second_ref)):
                expert, rank = slots(col_ref[...], ids[...], j, 2, cap)
                target = expert * rows + part * cap + rank
                one = jnp.where(iota((total, toks), 0) == target, 1.0, 0.0)
                hit = one if hit is None else hit + one
            hot_ref[:, part * toks : (part + 1) * toks] = hit.astype(BF)
        expert, rank = slots(col_ref[...], row_ref[...], 0, 1, cap)
        for part in range(ng):
            target = expert * rows + (nx + part) * cap + rank
            low = nx * toks + part * pairs
            hot_ref[:, low : low + pairs] = onehot(iota((total, pairs), 0) == target)
        row = iota((total, pairs), 0)
        mine = (row >> (rows.bit_length() - 1)) == row_ref[...]
        marked = (row & (rows - 1)) == (nx + ng) * cap
        add_ref[...] = jnp.sum(jnp.where(mine & marked, 1.0, 0.0), axis=1, keepdims=True)

    data = jnp.concatenate(
        [x_ref[:, p * 128 : (p + 1) * 128] for p in range(nx)]
        + [g_ref[:, p * 128 : (p + 1) * 128] for p in range(ng)],
        0,
    )
    out = jnp.dot(hot_ref[...], data, preferred_element_type=F32) + add_ref[...]
    out_ref[...] = out.astype(BF).reshape(groups, rows, 128)[None]


def inverse_kernel(cap, nx, ng, lev_ref, in_ref, a_ref, s_ref, h_ref, x_ref, m_ref):
    shards, groups, rows, _ = in_ref.shape
    live = groups * cap
    shape = (live, groups * rows)
    row = iota(shape, 0)
    source = div(row, cap)
    base = source * rows + (row - source * cap)
    pick = jnp.concatenate(
        [onehot(iota(shape, 1) == base + part * cap) for part in range(nx + ng)], 0
    )
    total = jnp.zeros((1, 128), F32)
    mark = (nx + ng) * cap
    for s in range(shards):
        data = in_ref[s].reshape(groups * rows, 128)
        got = jnp.dot(pick, data, preferred_element_type=F32).astype(BF)
        for part in range(nx + ng):
            piece = got[part * live : (part + 1) * live]
            if part < nx:
                x_ref[s * live : (s + 1) * live, part * 128 : (part + 1) * 128] = piece
            else:
                h_ref[s, :, (part - nx) * 128 : (part - nx + 1) * 128] = piece
        for g in range(groups):
            total = total + in_ref[s, g, mark : mark + 1, :].astype(F32)
    scale = 1.0 / total[:, :1]
    eye = iota((BLK, BLK), 0) == iota((BLK, BLK), 1)
    width = h_ref.shape[2]
    h = h_ref[...].reshape(shards * live, width)
    for m in range(1 + width // BLK):
        part = x_ref[...] if m == 0 else h[:, (m - 1) * BLK : m * BLK]
        cov = lax.dot_general(part, part, TN, preferred_element_type=F32)
        damp = 0.05 * jnp.exp(0.4 * jnp.full((1, 1), lev_ref[m], F32))
        m_ref[m] = cov * scale + jnp.where(eye, damp, 0.0)
    invert_all(m_ref, m_ref.shape[0])
    a_ref[...] = -m_ref[0]
    s_ref[...] = -m_ref[1:]


def product_kernel(block_ref, x_ref, h_ref, a_ref, s_ref, out_ref, sum_ref):
    step = pl.program_id(0)
    shards, live, width = h_ref.shape
    h = h_ref[...].reshape(shards * live, width)
    x = x_ref[...].reshape(shards * live, BLK)
    gradient = lax.dot_general(x, h, TN, preferred_element_type=F32)
    left = split2(a_ref[0])
    total = jnp.zeros((8, 128), F32)
    for c in range(width // BLK):
        cut = slice(c * BLK, (c + 1) * BLK)
        right = dot3(split2(gradient[:, cut]), split2(s_ref[c]))
        out = dot3(left, split2(right))
        out_ref[:, cut] = out
        square = (out * out).reshape(BLK // 8, 8, BLK).sum(axis=0)
        for k in range(BLK // 128):
            total = total + square[:, k * 128 : (k + 1) * 128]

    @pl.when(step == 0)
    def _():
        sum_ref[...] = jnp.zeros_like(sum_ref)

    sum_ref[...] += total


def scale_kernel(count, norm_ref, in_ref, out_ref):
    total = jnp.sum(jnp.sum(norm_ref[...], axis=0, keepdims=True), axis=1, keepdims=True)
    out_ref[...] = (in_ref[...] * lax.rsqrt(total / count + 1e-06)).astype(BF)


def shift(n, rest, by, inner):
    pairs = []
    for hi in range(n):
        for lo in range(rest):
            src = hi * rest + lo
            if inner:
                pairs.append((src, hi * rest + (lo + by) % rest))
            else:
                pairs.append((src, ((hi + by) % n) * rest + lo))
    return pairs


def full(shape):
    return pl.BlockSpec(shape, lambda *_: (0,) * len(shape))


def local(tokens_in, out_grad, expert_ids, d_levels, f_levels):
    groups, shards = lax.axis_size("expert"), lax.axis_size("shard")
    toks, width = tokens_in.shape
    ff = out_grad.shape[2]
    ff_dev = ff // shards
    cap = min(toks, max(2, 5 * toks // (2 * groups)))
    live = groups * cap
    own = width // shards
    parts = 4
    nx, ng = own // 128, ff_dev // 128
    rows = 64
    call = functools.partial(pl.pallas_call, compiler_params=PARAMS)

    id_row = expert_ids.reshape(1, 2 * toks)
    id_col = expert_ids.reshape(2 * toks, 1)
    first, second = expert_ids[:, 0].reshape(1, toks), expert_ids[:, 1].reshape(1, toks)

    x_send = call(
        functools.partial(send_x_kernel, cap, parts),
        out_shape=jax.ShapeDtypeStruct((groups * cap * parts, width // parts), BF),
        name="send_x",
    )(id_col, first, second, tokens_in)
    x_recv = lax.all_to_all(
        x_send.reshape(groups, cap * parts, width // parts), "expert", 0, 0, tiled=True
    )
    x_group = call(
        functools.partial(take_x_kernel, cap, parts),
        out_shape=jax.ShapeDtypeStruct((live, width), BF),
        name="take_x",
    )(x_recv)
    rows_x = lax.all_gather(x_group[None], "shard", axis=0, tiled=True)

    payload = call(
        functools.partial(payload_kernel, cap, rows, nx, ng),
        out_shape=jax.ShapeDtypeStruct((shards, groups, rows, 128), BF),
        grid=(shards,),
        in_specs=[
            full((2 * toks, 1)),
            full((1, 2 * toks)),
            full((1, toks)),
            full((1, toks)),
            pl.BlockSpec((toks, own), lambda s: (0, s)),
            pl.BlockSpec((2 * toks, ff_dev), lambda s: (0, s)),
        ],
        out_specs=pl.BlockSpec((1, groups, rows, 128), lambda s: (s, 0, 0, 0)),
        scratch_shapes=[
            pltpu.VMEM((groups * rows, nx * toks + ng * 2 * toks), BF),
            pltpu.VMEM((groups * rows, 1), F32),
        ],
        name="payload",
    )(id_col, id_row, first, second, tokens_in, out_grad.reshape(2 * toks, ff))
    received = lax.all_to_all(
        payload.reshape(shards * groups, rows, 128), ("shard", "expert"), 0, 0, tiled=True
    ).reshape(shards, groups, rows, 128)

    me = lax.axis_index("shard")
    levels = jnp.concatenate(
        [lax.dynamic_slice_in_dim(d_levels[0], me, 1, 0), f_levels[0]]
    ).astype(F32)
    vm = pl.BlockSpec(memory_space=pltpu.VMEM)
    inv_a, inv_f, rows_g = call(
        functools.partial(inverse_kernel, cap, nx, ng),
        out_shape=(
            jax.ShapeDtypeStruct((BLK, BLK), F32),
            jax.ShapeDtypeStruct((ff_dev // BLK, BLK, BLK), F32),
            jax.ShapeDtypeStruct((shards, live, ff_dev), BF),
        ),
        in_specs=[pl.BlockSpec(memory_space=pltpu.SMEM), vm],
        out_specs=(vm, vm, vm),
        scratch_shapes=[
            pltpu.VMEM((shards * live, own), BF),
            pltpu.VMEM((1 + ff_dev // BLK, BLK, BLK), F32),
        ],
        name="inverse",
    )(levels, received)

    side = 4
    outer = shards // side
    send = functools.partial(lax.ppermute, axis_name="shard")
    line = jnp.stack(
        [inv_a] + [send(inv_a, perm=shift(outer, side, k, True)) for k in range(1, side)]
    )
    plane = jnp.concatenate(
        [line] + [send(line, perm=shift(outer, side, k, False)) for k in range(1, outer)], 0
    )
    order = jnp.arange(shards, dtype=jnp.int32)
    up, across = order // side, order % side
    block_of = ((me // side - up) % outer) * side + (me % side - across) % side

    precond, square = call(
        product_kernel,
        out_shape=(
            jax.ShapeDtypeStruct((width, ff_dev), F32),
            jax.ShapeDtypeStruct((8, 128), F32),
        ),
        grid_spec=pltpu.PrefetchScalarGridSpec(
            num_scalar_prefetch=1,
            grid=(shards,),
            in_specs=[
                pl.BlockSpec((shards, live, BLK), lambda i, b: (0, 0, b[i])),
                full((shards, live, ff_dev)),
                pl.BlockSpec((1, BLK, BLK), lambda i, b: (i, 0, 0)),
                full((ff_dev // BLK, BLK, BLK)),
            ],
            out_specs=(
                pl.BlockSpec((BLK, ff_dev), lambda i, b: (b[i], 0)),
                full((8, 128)),
            ),
        ),
        name="product",
    )(block_of, rows_x, rows_g, plane, inv_f)

    norm = jnp.sum(square, axis=0, keepdims=True)
    norm = lax.all_to_all(jnp.broadcast_to(norm, (groups, 128)), "expert", 0, 0, tiled=True)
    norm = jnp.sum(norm, axis=0, keepdims=True)
    norm = lax.all_to_all(jnp.broadcast_to(norm, (shards, 128)), "shard", 0, 0, tiled=True)
    tile = width // 8
    ascent = call(
        functools.partial(scale_kernel, float(groups * width * ff)),
        out_shape=jax.ShapeDtypeStruct((width, ff_dev), BF),
        grid=(8,),
        in_specs=[full((shards, 128)), pl.BlockSpec((tile, ff_dev), lambda i: (i, 0))],
        out_specs=pl.BlockSpec((tile, ff_dev), lambda i: (i, 0)),
        name="scale",
    )(norm, precond)
    return ascent[None]


def solution(mesh):
    return jax.shard_map(
        local,
        mesh=mesh,
        in_specs=(
            P(("expert", "shard"), None),
            P(("expert", "shard"), None, None),
            P(("expert", "shard"), None),
            P("expert", None),
            P("expert", "shard"),
        ),
        out_specs=P("expert", None, "shard"),
        check_vma=False,
    )
```

time: 563 us -> 244 us (0.43)
  other arithmetic: 220 us -> 3.45 us
  blocking collectives: 121 us -> 37.2 us
  local copies, waits for them, and re-layouts: 84.3 us -> 13.4 us
  Pallas kernels: 0 us -> 67.9 us
  matrix products: 56.6 us -> 0 us
  waiting for transfers between devices: 44.2 us -> 93.1 us
    another operation x23 -> x1, other arithmetic: 164 us -> 1.02 us  [local(): jnp.stack([inv_a] + [send(inv_a, perm=shift(outer, side, k, True)) for k...]
    pallas_call x0 -> x6, Pallas kernels: none -> 67.9 us  [the longest x1 25.1 us: local(): call(product_kernel, out_shape=(jax.ShapeDtypeStruct((width, ff_dev), F32...]
    psum x1 -> x0, blocking collectives: 65 us -> none  [local(): norm_total = lax.psum(jnp.sum(precond * precond), ('expert', 'shard'))]
    ppermute x0 -> x6, waiting for transfers between devices: none -> 64.4 us  [the longest x3 42.2 us: local(): send(line, perm=shift(outer, side, k, False))]
    dot_general x7 -> x0, matrix products: 51.5 us -> none  [the longest x1 18.4 us: local(): jnp.einsum('dcj,cjk->dck', left_done.reshape(width, ff_dev // BLK, BLK),...]
    unnamed x3 -> x0, other arithmetic: 45.2 us -> none
    unnamed x1 -> x0, blocking collectives: 35.3 us -> none
    all_gather x2 -> x1, waiting for transfers between devices: 29.6 us -> 0.01 us  [local(): rows_x = lax.all_gather(x_group[None], 'shard', axis=0, tiled=True)]
  transfers between devices with their start and end apart: 5 -> 8, of which waited for: 2 -> 6; matrix products, arithmetic and copies ran while one was open for 53% -> 5% of each run, Pallas kernels for 0% -> 12%
where the time goes in v1:
time: 244 us; the launch traced here: 242 us
  waiting for transfers between devices  93.1 us (38%)
  Pallas kernels  67.9 us (28%)
  blocking collectives  37.2 us (15%)
  local copies, waits for them, and re-layouts  13.4 us (5%)
  between operations  13.4 us (5%)
  starting transfers between devices  13.2 us (5%)
  other arithmetic  3.45 us (1%)
    ppermute x3, waiting for transfers between devices, local(): send(line, perm=shift(outer, side, k, False))  42.2 us
    all_to_all x1, waiting for transfers between devices, local(): lax.all_to_all(payload.reshape(shards * groups, rows, 128), ('shard', 'ex...  28.7 us
    pallas_call x1, Pallas kernels, local(): call(product_kernel, out_shape=(jax.ShapeDtypeStruct((width, ff_dev), F32...  25.1 us
    ppermute x3, waiting for transfers between devices, local(): send(inv_a, perm=shift(outer, side, k, True))  22.2 us
    pallas_call x1, Pallas kernels, local(): call(functools.partial(inverse_kernel, cap, nx, ng), out_shape=(jax.Shape...  18.3 us
    all_to_all x1, blocking collectives, local(): lax.all_to_all(x_send.reshape(groups, cap * parts, width // parts), 'expe...  16.8 us
    pallas_call x1, Pallas kernels, local(): call(functools.partial(payload_kernel, cap, rows, nx, ng), out_shape=jax....  11.4 us
    all_to_all x1, blocking collectives, local(): lax.all_to_all(jnp.broadcast_to(norm, (groups, 128)), 'expert', 0, 0, til...  10.3 us
  transfers between devices with their start and end apart: 8, of which 6 were waited for; matrix products, arithmetic and copies ran while one was open for 5% of the time, Pallas kernels for 12%

profile of v1, /device:TPU:1, one launch (start us, length us, event | category | flops | bytes accessed | tf_op | source)
XLA Modules:
  0.0 241.7 jit_solution(14694072599370165206)
XLA Ops:
  6.5 1.3 slice_bitcast_fusion
  7.8 0.8 copy.22
  8.6 0.7 reshape.38.col_ref
  9.3 2.3 send_x.1
  11.6 16.8 %all_to_all.24.in_ref = bf16[8,40,1024]{2,1,0:T(8,128)(2,1)} all-to-all(bf16[8,40,1024]{2,1,0:T(8,128)(2,1)} %bitcast.24), channel_id=1, replica_groups=mesh['expert'=8,'shard'=16] {'expert'}, dimensions={0} | all-to-all | bytes 1310720 | tf_op jit(solution)/shard_map/all_to_all | solution.py:291
  28.4 2.6 %take_x.1 = bf16[80,4096]{1,0:T(8,128)(2,1)} custom-call(bf16[8,40,1024]{2,1,0:T(8,128)(2,1)} %all_to_all.24.in_ref), custom_call_target="tpu_custom_call" | custom-call | tf_op jit(solution)/shard_map/take_x/pallas_call | solution.py:294
  31.7 1.2 reshape.34.g_ref
  32.9 11.4 %payload.1 = bf16[16,8,64,128]{3,2,1,0:T(8,128)(2,1)} custom-call(s32[64,1]{1,0:T(8,128)} %reshape.38.col_ref, s32[1,64]{1,0:T(1,128)} %reshape.33.row_ref, s32[1,32]{1,0:T(1,128)} %get-tuple-element.16.first_ref, s32[1,32]{1,0:T(1,128)} %get-tuple-element.15.second_ref, bf16[32,4096]{1,0:T(8,128)(2,1)} %x_ref.3, bf16[64,8192]{1,0:T(8,128)(2,1)} %reshape.34.g_ref), custom_call_target="tpu_custom_call" | custom-call | tf_op jit(solution)/shard_map/payload/pallas_call | solution.py:301
  44.3 9.0 %all-to-all-start.1 = ((bf16[128,64,128]{2,1,0:T(8,128)(2,1)}), bf16[128,64,128]{2,1,0:T(8,128)(2,1)S(1)}, u32[]{:S(2)}, u32[]{:S(2)}) async-start(bf16[128,64,128]{2,1,0:T(8,128)(2,1)} %bitcast.23), calls=%async_computation.1 | async-start | bytes 4194304 | tf_op jit(solution)/shard_map/all_to_all | solution.py:320
  53.9 1.2 add_convert_fusion.lev_ref
  55.1 28.7 %all-to-all-done.1 = bf16[128,64,128]{2,1,0:T(8,128)(2,1)S(1)} async-done(((bf16[128,64,128]{2,1,0:T(8,128)(2,1)}), bf16[128,64,128]{2,1,0:T(8,128)(2,1)S(1)}, u32[]{:S(2)}, u32[]{:S(2)}) %all-to-all-start.1) | async-done | bytes 2097184 | tf_op jit(solution)/shard_map/all_to_all | solution.py:320
  83.8 1.3 copy-done.1
  85.1 18.3 %inverse.1 = (f32[256,256]{1,0:T(8,128)}, f32[2,256,256]{2,1,0:T(8,128)}, bf16[16,80,512]{2,1,0:T(8,128)(2,1)}) custom-call(f32[3]{0:T(128)} %add_convert_fusion.lev_ref, bf16[16,8,64,128]{3,2,1,0:T(8,128)(2,1)} %bitcast.22), custom_call_target="tpu_custom_call" | custom-call | tf_op jit(solution)/shard_map/inverse/pallas_call | solution.py:329
  104.9 12.3 %collective-permute-done.2 = f32[256,256]{1,0:T(8,128)S(1)} collective-permute-done((f32[256,256]{1,0:T(8,128)}, f32[256,256]{1,0:T(8,128)S(1)}, u32[]{:S(2)}, u32[]{:S(2)}) %collective-permute-start.2) | collective-permute-done | bytes 262176 | tf_op jit(solution)/shard_map/ppermute | solution.py:349
  117.2 1.8 collective-permute-done.1
  119.1 8.0 %collective-permute-done = f32[256,256]{1,0:T(8,128)S(1)} collective-permute-done((f32[256,256]{1,0:T(8,128)}, f32[256,256]{1,0:T(8,128)S(1)}, u32[]{:S(2)}, u32[]{:S(2)}) %collective-permute-start) | collective-permute-done | bytes 262176 | tf_op jit(solution)/shard_map/ppermute | solution.py:349
  127.1 1.0 pad_maximum_fusion
  129.3 2.1 collective-permute-start.5
  131.4 1.7 constant_dynamic-update-slice_fusion.6
  133.1 0.7 constant_dynamic-update-slice_fusion.5
  133.8 0.7 constant_dynamic-update-slice_fusion.4
  134.5 0.7 constant_dynamic-update-slice_fusion.3
  135.2 20.9 %collective-permute-done.3 = f32[4,256,256]{2,1,0:T(8,128)S(1)} collective-permute-done((f32[4,256,256]{2,1,0:T(8,128)S(1)}, f32[4,256,256]{2,1,0:T(8,128)S(1)}, u32[]{:S(2)}, u32[]{:S(2)}) %collective-permute-start.3) | collective-permute-done | bytes 1048608 | tf_op jit(solution)/shard_map/ppermute | solution.py:352
  156.1 1.0 constant_dynamic-update-slice_fusion.2
  157.1 21.3 %collective-permute-done.4 = f32[4,256,256]{2,1,0:T(8,128)S(1)} collective-permute-done((f32[4,256,256]{2,1,0:T(8,128)S(1)}, f32[4,256,256]{2,1,0:T(8,128)S(1)}, u32[]{:S(2)}, u32[]{:S(2)}) %collective-permute-start.4) | collective-permute-done | bytes 1048608 | tf_op jit(solution)/shard_map/ppermute | solution.py:352
  178.5 1.0 constant_dynamic-update-slice_fusion.1
  179.5 1.0 constant_dynamic-update-slice_fusion.a_ref
  180.5 25.1 %product.1 = (f32[4096,512]{1,0:T(8,128)}, f32[8,128]{1,0:T(8,128)}) custom-call(s32[16]{0:T(128)} %fusion.1.block_ref, bf16[16,80,4096]{2,1,0:T(8,128)(2,1)} %bitcast.21, bf16[16,80,512]{2,1,0:T(8,128)(2,1)} %get-tuple-element.10.h_ref, f32[16,256,256]{2,1,0:T(8,128)} %constant_dynamic-update-slice_fusion.a_ref, f32[2,256,256]{2,1,0:T(8,128)} %get-tuple-element.12.s_ref), custom_call_target="tpu_custom_call" | custom-call | tf_op jit(solution)/shard_map/product/pallas_call | solution.py:358
  205.6 0.7 reduce_sum.18
  206.4 10.3 %all_to_all.25 = f32[8,1,128]{2,1,0:T(1,128)S(1)} all-to-all(f32[8,1,128]{2,1,0:T(1,128)S(1)} %broadcast_in_dim.9), channel_id=1, replica_groups=mesh['expert'=8,'shard'=16] {'expert'}, dimensions={0} | all-to-all | bytes 8192 | tf_op jit(solution)/shard_map/all_to_all | solution.py:382
  216.7 10.1 %all_to_all.26 = f32[16,1,128]{2,1,0:T(1,128)} all-to-all(f32[16,1,128]{2,1,0:T(1,128)S(1)} %broadcast_in_dim.20), channel_id=1, replica_groups=mesh['expert'=8,'shard'=16] {'shard'}, dimensions={0} | all-to-all | bytes 16384 | tf_op jit(solution)/shard_map/all_to_all | solution.py:384
  226.7 8.2 %scale.1 = bf16[4096,512]{1,0:T(8,128)(2,1)} custom-call(f32[16,128]{1,0:T(8,128)} %bitcast.29, f32[4096,512]{1,0:T(8,128)} %get-tuple-element.14.in_ref), custom_call_target="tpu_custom_call" | custom-call | tf_op jit(solution)/shard_map/scale/pallas_call | solution.py:386
  (22 shorter events, 3.9 us)
Async XLA Ops:
  6.5 46.8 %copy-start = (s32[1,16]{1,0:T(1,128)S(1)}, s32[1,16]{1,0:T(1,128)}, u32[]{:S(2)}) copy-start(s32[1,16]{1,0:T(1,128)} %param.8) | copy-start | bytes 196
  6.5 25.1 %copy-start.2 = (bf16[32,2,8192]{2,1,0:T(2,128)(2,1)S(1)}, bf16[32,2,8192]{2,1,0:T(2,128)(2,1)}, u32[]{:S(2)}) copy-start(bf16[32,2,8192]{2,1,0:T(2,128)(2,1)} %param.6) | copy-start | bytes 3145732
  6.5 174.0 %all-gather.3.cloned.1.call-start = ((), (), s32[]{:S(2)}) async-start(), calls=%async_computation.4 | async-start | bytes 11141120 | tf_op jit(solution)/shard_map/all_gather | solution.py:299
  32.9 21.1 %copy-start.3 = (s32[1,2]{1,0:T(1,128)S(1)}, s32[1,2]{1,0:T(1,128)}, u32[]{:S(2)}) copy-start(s32[1,2]{1,0:T(1,128)} %param.9) | copy-start | bytes 28
  44.3 39.5 %all-to-all-start.1 = ((bf16[128,64,128]{2,1,0:T(8,128)(2,1)}), bf16[128,64,128]{2,1,0:T(8,128)(2,1)S(1)}, u32[]{:S(2)}, u32[]{:S(2)}) async-start(bf16[128,64,128]{2,1,0:T(8,128)(2,1)} %bitcast.23), calls=%async_computation.1 | async-start | bytes 4194304 | tf_op jit(solution)/shard_map/all_to_all | solution.py:320
  83.8 1.3 copy-start.1
  103.4 13.8 %collective-permute-start.2 = (f32[256,256]{1,0:T(8,128)}, f32[256,256]{1,0:T(8,128)S(1)}, u32[]{:S(2)}, u32[]{:S(2)}) collective-permute-start(f32[256,256]{1,0:T(8,128)} %get-tuple-element.11), channel_id=1, source_target_pairs={{0,3},{1,0},{2,1},{3,2},{4,7},{5,4},{6,5},{7,6},{8,11},{9,8},{10,9... | collective-permute-start | bytes 786440 | tf_op jit(solution)/shard_map/ppermute | solution.py:349
  103.9 15.1 %collective-permute-start.1 = (f32[256,256]{1,0:T(8,128)}, f32[256,256]{1,0:T(8,128)S(1)}, u32[]{:S(2)}, u32[]{:S(2)}) collective-permute-start(f32[256,256]{1,0:T(8,128)} %get-tuple-element.11), channel_id=1, source_target_pairs={{0,2},{1,3},{2,0},{3,1},{4,6},{5,7},{6,4},{7,5},{8,10},{9,11},{10,... | collective-permute-start | bytes 786440 | tf_op jit(solution)/shard_map/ppermute | solution.py:349
  104.6 22.5 %collective-permute-start = (f32[256,256]{1,0:T(8,128)}, f32[256,256]{1,0:T(8,128)S(1)}, u32[]{:S(2)}, u32[]{:S(2)}) collective-permute-start(f32[256,256]{1,0:T(8,128)} %get-tuple-element.11), channel_id=1, source_target_pairs={{0,1},{1,2},{2,3},{3,0},{4,5},{5,6},{6,7},{7,4},{8,9},{9,10},{10,1... | collective-permute-start | bytes 786440 | tf_op jit(solution)/shard_map/ppermute | solution.py:349
  128.1 28.0 %collective-permute-start.3 = (f32[4,256,256]{2,1,0:T(8,128)S(1)}, f32[4,256,256]{2,1,0:T(8,128)S(1)}, u32[]{:S(2)}, u32[]{:S(2)}) collective-permute-start(f32[4,256,256]{2,1,0:T(8,128)S(1)} %pad_maximum_fusion), channel_id=1, source_target_pairs={{0,4},{1,5},{2,6},{3,7},{4,8},{5,9},{6,10},{7,11},{8,12},{9,13},{1... | collective-permute-start | bytes 3145736 | tf_op jit(solution)/shard_map/ppermute | solution.py:352
  129.3 50.2 %collective-permute-start.5 = (f32[4,256,256]{2,1,0:T(8,128)S(1)}, f32[4,256,256]{2,1,0:T(8,128)S(1)}, u32[]{:S(2)}, u32[]{:S(2)}) collective-permute-start(f32[4,256,256]{2,1,0:T(8,128)S(1)} %pad_maximum_fusion), channel_id=1, source_target_pairs={{0,12},{1,13},{2,14},{3,15},{4,0},{5,1},{6,2},{7,3},{8,4},{9,5},{1... | collective-permute-start | bytes 3145736 | tf_op jit(solution)/shard_map/ppermute | solution.py:352
  131.4 47.1 %collective-permute-start.4 = (f32[4,256,256]{2,1,0:T(8,128)S(1)}, f32[4,256,256]{2,1,0:T(8,128)S(1)}, u32[]{:S(2)}, u32[]{:S(2)}) collective-permute-start(f32[4,256,256]{2,1,0:T(8,128)S(1)} %pad_maximum_fusion), channel_id=1, source_target_pairs={{0,8},{1,9},{2,10},{3,11},{4,12},{5,13},{6,14},{7,15},{8,0},{9,1},... | collective-permute-start | bytes 3145736 | tf_op jit(solution)/shard_map/ppermute | solution.py:352
Sparse Core Ops, SparseCore 0:
  31.2 113.6 all-gather.2

commit v2 on v1

--- a/solution.py
+++ b/solution.py
@@ -13,8 +13,6 @@
 F32 = jnp.float32
 BF = jnp.bfloat16
 TN = (((0,), (0,)), ((), ()))
-VMEM = 56 << 20
-PARAMS = pltpu.CompilerParams(vmem_limit_bytes=VMEM)
 
 
 def iota(shape, dim):
@@ -135,7 +133,7 @@
     ).astype(BF)
 
 
-def take_x_kernel(cap, parts, in_ref, out_ref):
+def take_x_kernel(cap, parts, in_ref, *out_refs):
     groups, per, width = in_ref.shape
     data = in_ref[...].reshape(groups * per, width)
     shape = (groups * cap, groups * per)
@@ -144,7 +142,8 @@
     base = source * per + (row - source * cap)
     for part in range(parts):
         pick = onehot(iota(shape, 1) == base + part * cap)
-        out_ref[:, part * width : (part + 1) * width] = jnp.dot(
+        half, at = divmod(part, parts // len(out_refs))
+        out_refs[half][:, at * width : (at + 1) * width] = jnp.dot(
             pick, data, preferred_element_type=F32
         ).astype(BF)
 
@@ -175,17 +174,24 @@
         marked = (row & (rows - 1)) == (nx + ng) * cap
         add_ref[...] = jnp.sum(jnp.where(mine & marked, 1.0, 0.0), axis=1, keepdims=True)
 
+    pair = out_ref.shape[0]
+
+    def lanes(ref, part, each):
+        cuts = [(t * each + part) * 128 for t in range(pair)]
+        return jnp.concatenate([ref[:, at : at + 128] for at in cuts], 1)
+
     data = jnp.concatenate(
-        [x_ref[:, p * 128 : (p + 1) * 128] for p in range(nx)]
-        + [g_ref[:, p * 128 : (p + 1) * 128] for p in range(ng)],
-        0,
+        [lanes(x_ref, p, nx) for p in range(nx)] + [lanes(g_ref, p, ng) for p in range(ng)], 0
     )
     out = jnp.dot(hot_ref[...], data, preferred_element_type=F32) + add_ref[...]
-    out_ref[...] = out.astype(BF).reshape(groups, rows, 128)[None]
-
-
-def inverse_kernel(cap, nx, ng, lev_ref, in_ref, a_ref, s_ref, h_ref, x_ref, m_ref):
-    shards, groups, rows, _ = in_ref.shape
+    for t in range(pair):
+        piece = out[:, t * 128 : (t + 1) * 128].astype(BF)
+        out_ref[t] = piece.reshape(groups, rows, 128)
+
+
+def inverse_kernel(cap, nx, ng, rel_ref, lev_ref, in_ref, q_ref, p_ref, s_ref, one_ref, two_ref,
+                   x_ref, m_ref):
+    groups, shards, rows, _ = in_ref.shape
     live = groups * cap
     shape = (live, groups * rows)
     row = iota(shape, 0)
@@ -197,69 +203,107 @@
     total = jnp.zeros((1, 128), F32)
     mark = (nx + ng) * cap
     for s in range(shards):
-        data = in_ref[s].reshape(groups * rows, 128)
+        data = in_ref[:, s].reshape(groups * rows, 128)
         got = jnp.dot(pick, data, preferred_element_type=F32).astype(BF)
-        for part in range(nx + ng):
-            piece = got[part * live : (part + 1) * live]
-            if part < nx:
-                x_ref[s * live : (s + 1) * live, part * 128 : (part + 1) * 128] = piece
-            else:
-                h_ref[s, :, (part - nx) * 128 : (part - nx + 1) * 128] = piece
+        for part in range(nx):
+            x_ref[s * live : (s + 1) * live, part * 128 : (part + 1) * 128] = got[
+                part * live : (part + 1) * live
+            ]
+        h = jnp.concatenate(
+            [got[part * live : (part + 1) * live] for part in range(nx, nx + ng)], 1
+        )
+        one_ref[rel_ref[s]] = h
+        two_ref[rel_ref[shards + s]] = h
         for g in range(groups):
-            total = total + in_ref[s, g, mark : mark + 1, :].astype(F32)
+            total = total + in_ref[g, s, mark : mark + 1, :].astype(F32)
     scale = 1.0 / total[:, :1]
     eye = iota((BLK, BLK), 0) == iota((BLK, BLK), 1)
-    width = h_ref.shape[2]
-    h = h_ref[...].reshape(shards * live, width)
+    width = one_ref.shape[2]
+    h = one_ref[...].reshape(shards * live, width)
     for m in range(1 + width // BLK):
         part = x_ref[...] if m == 0 else h[:, (m - 1) * BLK : m * BLK]
         cov = lax.dot_general(part, part, TN, preferred_element_type=F32)
         damp = 0.05 * jnp.exp(0.4 * jnp.full((1, 1), lev_ref[m], F32))
         m_ref[m] = cov * scale + jnp.where(eye, damp, 0.0)
     invert_all(m_ref, m_ref.shape[0])
-    a_ref[...] = -m_ref[0]
     s_ref[...] = -m_ref[1:]
-
-
-def product_kernel(block_ref, x_ref, h_ref, a_ref, s_ref, out_ref, sum_ref):
-    step = pl.program_id(0)
-    shards, live, width = h_ref.shape
-    h = h_ref[...].reshape(shards * live, width)
-    x = x_ref[...].reshape(shards * live, BLK)
-    gradient = lax.dot_general(x, h, TN, preferred_element_type=F32)
-    left = split2(a_ref[0])
+    half = BLK // 2
+    top, low = -m_ref[0, :half, :half], -m_ref[0, half:, half:]
+    down, across = iota((half, half), 0), iota((half, half), 1)
+    q_ref[:half] = -m_ref[0, :half, half:]
+    diag = jnp.sum(jnp.where(down == across, low, 0.0), axis=0, keepdims=True)
+    q_ref[half:] = jnp.broadcast_to(diag, (8, half))
+    p_ref[...] = jnp.where(down >= across, top, low)
+
+
+def unfold(q_ref, p_ref):
+    half = p_ref.shape[1]
+    quarter, diag, both = q_ref[0, :half], q_ref[0, half : half + 1], p_ref[0]
+    down, across = iota((half, half), 0), iota((half, half), 1)
+    lower = jnp.where(down > across, both, 0.0)
+    upper = jnp.where(down < across, both, 0.0)
+    eye = down == across
+    top = lower + lower.T + jnp.where(eye, both, 0.0)
+    low = upper + upper.T + jnp.where(eye, diag, 0.0)
+    return jnp.concatenate(
+        [jnp.concatenate([top, quarter], 1), jnp.concatenate([quarter.T, low], 1)], 0
+    )
+
+
+def product_kernel(pieces, rel_ref, *refs):
+    x_refs, refs = (refs[:pieces], refs[pieces : 2 * pieces]), refs[2 * pieces :]
+    h_refs, q_refs, p_refs = refs[0:2], refs[2:4], refs[4:6]
+    s_ref, out_refs, sum_ref = refs[6], refs[7:9], refs[9]
+    width = h_refs[0].shape[2]
     total = jnp.zeros((8, 128), F32)
-    for c in range(width // BLK):
-        cut = slice(c * BLK, (c + 1) * BLK)
-        right = dot3(split2(gradient[:, cut]), split2(s_ref[c]))
-        out = dot3(left, split2(right))
-        out_ref[:, cut] = out
-        square = (out * out).reshape(BLK // 8, 8, BLK).sum(axis=0)
-        for k in range(BLK // 128):
-            total = total + square[:, k * 128 : (k + 1) * 128]
-
-    @pl.when(step == 0)
+    for half in range(2):
+        x = jnp.concatenate([ref[...] for ref in x_refs[half]], 0)
+        h = h_refs[half][...].reshape(x.shape[0], width)
+        gradient = lax.dot_general(x, h, TN, preferred_element_type=F32)
+        left = split2(unfold(q_refs[half], p_refs[half]))
+        for c in range(width // BLK):
+            cut = slice(c * BLK, (c + 1) * BLK)
+            right = dot3(split2(gradient[:, cut]), split2(s_ref[c]))
+            out = dot3(left, split2(right))
+            out_refs[half][:, cut] = out
+            square = (out * out).reshape(BLK // 8, 8, BLK).sum(axis=0)
+            for k in range(BLK // 128):
+                total = total + square[:, k * 128 : (k + 1) * 128]
+
+    @pl.when(pl.program_id(0) == 0)
     def _():
         sum_ref[...] = jnp.zeros_like(sum_ref)
 
     sum_ref[...] += total
 
 
-def scale_kernel(count, norm_ref, in_ref, out_ref):
+def scale_kernel(count, norm_ref, one_ref, two_ref, out_ref):
     total = jnp.sum(jnp.sum(norm_ref[...], axis=0, keepdims=True), axis=1, keepdims=True)
-    out_ref[...] = (in_ref[...] * lax.rsqrt(total / count + 1e-06)).astype(BF)
-
-
-def shift(n, rest, by, inner):
+    scale = lax.rsqrt(total / count + 1e-06)
+    out_ref[0] = (one_ref[...] * scale).astype(BF)
+    out_ref[1] = (two_ref[...] * scale).astype(BF)
+
+
+SIDE = 4
+
+
+def send(array, by, inner):
     pairs = []
-    for hi in range(n):
-        for lo in range(rest):
-            src = hi * rest + lo
-            if inner:
-                pairs.append((src, hi * rest + (lo + by) % rest))
-            else:
-                pairs.append((src, ((hi + by) % n) * rest + lo))
-    return pairs
+    for at in range(SIDE * SIDE):
+        out, inn = at // SIDE, at % SIDE
+        if inner:
+            pairs.append((at, out * SIDE + (inn + by) % SIDE))
+        else:
+            pairs.append((at, (out + by) % SIDE * SIDE + inn))
+    return lax.ppermute(array, "shard", pairs)
+
+
+def gather(array, inner):
+    line = jnp.concatenate([array] + [send(array, k, inner) for k in range(1, SIDE)], 0)
+    half = line.shape[0] // 2
+    before, after = send(line, 1, not inner), send(line, SIDE - 1, not inner)
+    far = [send(before[:half], 1, not inner), send(after[half:], SIDE - 1, not inner)]
+    return [line, before, *far, after]
 
 
 def full(shape):
@@ -277,7 +321,10 @@
     parts = 4
     nx, ng = own // 128, ff_dev // 128
     rows = 64
-    call = functools.partial(pl.pallas_call, compiler_params=PARAMS)
+
+    def call(kernel, mib=16, **kwargs):
+        params = pltpu.CompilerParams(vmem_limit_bytes=mib << 20)
+        return pl.pallas_call(kernel, compiler_params=params, **kwargs)
 
     id_row = expert_ids.reshape(1, 2 * toks)
     id_col = expert_ids.reshape(2 * toks, 1)
@@ -291,92 +338,101 @@
     x_recv = lax.all_to_all(
         x_send.reshape(groups, cap * parts, width // parts), "expert", 0, 0, tiled=True
     )
-    x_group = call(
+    x_one, x_two = call(
         functools.partial(take_x_kernel, cap, parts),
-        out_shape=jax.ShapeDtypeStruct((live, width), BF),
+        out_shape=[jax.ShapeDtypeStruct((live, width // 2), BF)] * 2,
         name="take_x",
     )(x_recv)
-    rows_x = lax.all_gather(x_group[None], "shard", axis=0, tiled=True)
+    x_one, x_two = gather(x_one, True), gather(x_two, False)
 
     payload = call(
         functools.partial(payload_kernel, cap, rows, nx, ng),
         out_shape=jax.ShapeDtypeStruct((shards, groups, rows, 128), BF),
-        grid=(shards,),
+        grid=(shards // 2,),
         in_specs=[
             full((2 * toks, 1)),
             full((1, 2 * toks)),
             full((1, toks)),
             full((1, toks)),
-            pl.BlockSpec((toks, own), lambda s: (0, s)),
-            pl.BlockSpec((2 * toks, ff_dev), lambda s: (0, s)),
+            pl.BlockSpec((toks, 2 * own), lambda s: (0, s)),
+            pl.BlockSpec((2 * toks, 2 * ff_dev), lambda s: (0, s)),
         ],
-        out_specs=pl.BlockSpec((1, groups, rows, 128), lambda s: (s, 0, 0, 0)),
+        out_specs=pl.BlockSpec((2, groups, rows, 128), lambda s: (s, 0, 0, 0)),
         scratch_shapes=[
             pltpu.VMEM((groups * rows, nx * toks + ng * 2 * toks), BF),
             pltpu.VMEM((groups * rows, 1), F32),
         ],
         name="payload",
     )(id_col, id_row, first, second, tokens_in, out_grad.reshape(2 * toks, ff))
-    received = lax.all_to_all(
-        payload.reshape(shards * groups, rows, 128), ("shard", "expert"), 0, 0, tiled=True
-    ).reshape(shards, groups, rows, 128)
+    received = lax.all_to_all(payload, "shard", 0, 0, tiled=True).transpose(1, 0, 2, 3)
+    received = lax.all_to_all(received, "expert", 0, 0, tiled=True)
 
     me = lax.axis_index("shard")
+    order = jnp.arange(shards, dtype=jnp.int32)
+    back_out = (me // SIDE - order // SIDE) % SIDE
+    back_in = (me % SIDE - order % SIDE) % SIDE
+    place = jnp.concatenate([back_out * SIDE + back_in, back_in * SIDE + back_out])
     levels = jnp.concatenate(
         [lax.dynamic_slice_in_dim(d_levels[0], me, 1, 0), f_levels[0]]
     ).astype(F32)
-    vm = pl.BlockSpec(memory_space=pltpu.VMEM)
-    inv_a, inv_f, rows_g = call(
+    vm, sm = pl.BlockSpec(memory_space=pltpu.VMEM), pl.BlockSpec(memory_space=pltpu.SMEM)
+    half = BLK // 2
+    quarter, folded, inv_f, *rows_g = call(
         functools.partial(inverse_kernel, cap, nx, ng),
+        mib=24,
         out_shape=(
-            jax.ShapeDtypeStruct((BLK, BLK), F32),
+            jax.ShapeDtypeStruct((half + 8, half), F32),
+            jax.ShapeDtypeStruct((half, half), F32),
             jax.ShapeDtypeStruct((ff_dev // BLK, BLK, BLK), F32),
             jax.ShapeDtypeStruct((shards, live, ff_dev), BF),
+            jax.ShapeDtypeStruct((shards, live, ff_dev), BF),
         ),
-        in_specs=[pl.BlockSpec(memory_space=pltpu.SMEM), vm],
-        out_specs=(vm, vm, vm),
+        in_specs=[sm, sm, vm],
+        out_specs=(vm,) * 5,
         scratch_shapes=[
             pltpu.VMEM((shards * live, own), BF),
             pltpu.VMEM((1 + ff_dev // BLK, BLK, BLK), F32),
         ],
         name="inverse",
-    )(levels, received)
-
-    side = 4
-    outer = shards // side
-    send = functools.partial(lax.ppermute, axis_name="shard")
-    line = jnp.stack(
-        [inv_a] + [send(inv_a, perm=shift(outer, side, k, True)) for k in range(1, side)]
-    )
-    plane = jnp.concatenate(
-        [line] + [send(line, perm=shift(outer, side, k, False)) for k in range(1, outer)], 0
-    )
-    order = jnp.arange(shards, dtype=jnp.int32)
-    up, across = order // side, order % side
-    block_of = ((me // side - up) % outer) * side + (me % side - across) % side
-
-    precond, square = call(
-        product_kernel,
+    )(place, levels, received)
+    quarter = jnp.concatenate(gather(quarter, True), 0).reshape(shards, half + 8, half)
+    folded = jnp.concatenate(gather(folded, False), 0).reshape(shards, half, half)
+
+    steps = shards // 2
+
+    def columns(pieces):
+        return [pl.BlockSpec((p.shape[0], BLK), lambda i, r: (0, i)) for p in pieces]
+
+    one, two, square = call(
+        functools.partial(product_kernel, len(x_one)),
+        mib=24,
         out_shape=(
-            jax.ShapeDtypeStruct((width, ff_dev), F32),
+            jax.ShapeDtypeStruct((width // 2, ff_dev), F32),
+            jax.ShapeDtypeStruct((width // 2, ff_dev), F32),
             jax.ShapeDtypeStruct((8, 128), F32),
         ),
         grid_spec=pltpu.PrefetchScalarGridSpec(
             num_scalar_prefetch=1,
-            grid=(shards,),
+            grid=(steps,),
             in_specs=[
-                pl.BlockSpec((shards, live, BLK), lambda i, b: (0, 0, b[i])),
+                *columns(x_one),
+                *columns(x_two),
                 full((shards, live, ff_dev)),
-                pl.BlockSpec((1, BLK, BLK), lambda i, b: (i, 0, 0)),
+                full((shards, live, ff_dev)),
+                pl.BlockSpec((1, half + 8, half), lambda i, r: (r[i], 0, 0)),
+                pl.BlockSpec((1, half + 8, half), lambda i, r: (r[steps + i], 0, 0)),
+                pl.BlockSpec((1, half, half), lambda i, r: (r[shards + i], 0, 0)),
+                pl.BlockSpec((1, half, half), lambda i, r: (r[shards + steps + i], 0, 0)),
                 full((ff_dev // BLK, BLK, BLK)),
             ],
             out_specs=(
-                pl.BlockSpec((BLK, ff_dev), lambda i, b: (b[i], 0)),
+                pl.BlockSpec((BLK, ff_dev), lambda i, r: (i, 0)),
+                pl.BlockSpec((BLK, ff_dev), lambda i, r: (i, 0)),
                 full((8, 128)),
             ),
         ),
         name="product",
-    )(block_of, rows_x, rows_g, plane, inv_f)
+    )(place, *x_one, *x_two, *rows_g, quarter, quarter, folded, folded, inv_f)
 
     norm = jnp.sum(square, axis=0, keepdims=True)
     norm = lax.all_to_all(jnp.broadcast_to(norm, (groups, 128)), "expert", 0, 0, tiled=True)
@@ -385,13 +441,14 @@
     tile = width // 8
     ascent = call(
         functools.partial(scale_kernel, float(groups * width * ff)),
-        out_shape=jax.ShapeDtypeStruct((width, ff_dev), BF),
-        grid=(8,),
-        in_specs=[full((shards, 128)), pl.BlockSpec((tile, ff_dev), lambda i: (i, 0))],
-        out_specs=pl.BlockSpec((tile, ff_dev), lambda i: (i, 0)),
+        out_shape=jax.ShapeDtypeStruct((2, width // 2, ff_dev), BF),
+        grid=(4,),
+        in_specs=[full((shards, 128))]
+        + [pl.BlockSpec((tile, ff_dev), lambda i: (i, 0))] * 2,
+        out_specs=pl.BlockSpec((2, tile, ff_dev), lambda i: (0, i, 0)),
         name="scale",
-    )(norm, precond)
-    return ascent[None]
+    )(norm, one, two)
+    return ascent.reshape(1, width, ff_dev)
 
 
 def solution(mesh):

time: 244 us -> 242 us (level)
  starting transfers between devices: 13.2 us -> 53.1 us
  Pallas kernels: 67.9 us -> 47.4 us
  local copies, waits for them, and re-layouts: 13.4 us -> 27.7 us
  between operations: 13.4 us -> 0.32 us
  waiting for transfers between devices: 93.1 us -> 81.8 us
  blocking collectives: 37.2 us -> 29.7 us
  other arithmetic: 3.45 us -> 0.87 us
    ppermute x6 -> x28, starting transfers between devices: 4.22 us -> 32.3 us  [send(): return lax.ppermute(array, 'shard', pairs)]
    all_to_all x1 -> x0, blocking collectives: 16.8 us -> none  [local(): lax.all_to_all(x_send.reshape(groups, cap * parts, width // parts), 'expe...]
    ppermute x6 -> x28, waiting for transfers between devices: 64.4 us -> 51 us  [send(): return lax.ppermute(array, 'shard', pairs)]
    all_to_all x1 -> x3, starting transfers between devices: 8.99 us -> 20.8 us  [the longest x1 7.77 us: local(): lax.all_to_all(payload, 'shard', 0, 0, tiled=True).transpose(1, 0, 2, 3)]
    unnamed x15 -> x37, local copies, waits for them, and re-layouts: 8 us -> 18 us
    pallas_call x3, Pallas kernels: 46 us -> 38.2 us  [the longest x1 20.9 us: local(): call(functools.partial(product_kernel, len(x_one)), mib=24, out_shape=(ja...]
    all_to_all x1, blocking collectives: 10.3 us -> 17.1 us  [local(): lax.all_to_all(jnp.broadcast_to(norm, (groups, 128)), 'expert', 0, 0, til...]
    pallas_call x1, Pallas kernels: 11.4 us -> 5.01 us  [local(): call(functools.partial(payload_kernel, cap, rows, nx, ng), out_shape=jax....]
  transfers between devices with their start and end apart: 8 -> 31, of which waited for: 6 -> 13; matrix products, arithmetic and copies ran while one was open for 5% -> 7% of each run, Pallas kernels for 12% -> 9%
where the time goes in v2:
time: 242 us; the launch traced here: 241 us
  waiting for transfers between devices  81.8 us (34%)
  starting transfers between devices  53.1 us (22%)
  Pallas kernels  47.4 us (20%)
  blocking collectives  29.7 us (12%)
  local copies, waits for them, and re-layouts  27.7 us (11%)
    ppermute x28, waiting for transfers between devices, send(): return lax.ppermute(array, 'shard', pairs)  51 us
    ppermute x28, starting transfers between devices, send(): return lax.ppermute(array, 'shard', pairs)  32.3 us
    pallas_call x1, Pallas kernels, local(): call(functools.partial(product_kernel, len(x_one)), mib=24, out_shape=(ja...  20.9 us
    all_to_all x1, waiting for transfers between devices, local(): lax.all_to_all(payload, 'shard', 0, 0, tiled=True).transpose(1, 0, 2, 3)  20.6 us
    unnamed x37, local copies, waits for them, and re-layouts  18 us
    all_to_all x1, blocking collectives, local(): lax.all_to_all(jnp.broadcast_to(norm, (groups, 128)), 'expert', 0, 0, til...  17.1 us
    pallas_call x1, Pallas kernels, local(): call(functools.partial(inverse_kernel, cap, nx, ng), mib=24, out_shape=(j...  16.1 us
    all_to_all x1, blocking collectives, local(): lax.all_to_all(jnp.broadcast_to(norm, (shards, 128)), 'shard', 0, 0, tile...  12.6 us
  transfers between devices with their start and end apart: 31, of which 13 were waited for; matrix products, arithmetic and copies ran while one was open for 7% of the time, Pallas kernels for 9%

profile of v2, /device:TPU:1, one launch (start us, length us, event | category | flops | bytes accessed | tf_op | source)
XLA Modules:
  0.0 240.9 jit_solution(16089588957269998831)
XLA Ops:
  3.9 5.8 %all-to-all-start = ((bf16[8,40,1024]{2,1,0:T(8,128)(2,1)}), bf16[8,40,1024]{2,1,0:T(8,128)(2,1)S(1)}, u32[]{:S(2)}, u32[]{:S(2)}) async-start(bf16[8,40,1024]{2,1,0:T(8,128)(2,1)} %bitcast.2), calls=%async_computation | async-start | bytes 1310720 | tf_op jit(solution)/shard_map/all_to_all | solution.py:338
  10.7 5.0 %payload.1 = bf16[16,8,64,128]{3,2,1,0:T(8,128)(2,1)} custom-call(s32[64,1]{1,0:T(8,128)S(1)} %reshape.41.col_ref, s32[1,64]{1,0:T(1,128)S(1)} %reshape.36.row_ref, s32[1,32]{1,0:T(1,128)S(1)} %get-tuple-element.42.first_ref, s32[1,32]{1,0:T(1,128)S(1)} %get-tuple-element.41.second_ref, bf16[32,4096]{1,0:T(8,128)(2,1)S(1)} %copy-done.6, ...), custom_call_target="tpu_custom_call" | custom-call | tf_op jit(solution)/shard_map/payload/pallas_call | solution.py:348
  15.7 4.9 %all-to-all-done.in_ref = bf16[8,40,1024]{2,1,0:T(8,128)(2,1)S(1)} async-done(((bf16[8,40,1024]{2,1,0:T(8,128)(2,1)}), bf16[8,40,1024]{2,1,0:T(8,128)(2,1)S(1)}, u32[]{:S(2)}, u32[]{:S(2)}) %all-to-all-start) | async-done | bytes 655392 | tf_op jit(solution)/shard_map/all_to_all | solution.py:338
  20.6 7.8 %all-to-all-start.1 = ((bf16[16,8,64,128]{3,2,1,0:T(8,128)(2,1)}), bf16[16,8,64,128]{3,2,1,0:T(8,128)(2,1)S(1)}, u32[]{:S(2)}, u32[]{:S(2)}) async-start(bf16[16,8,64,128]{3,2,1,0:T(8,128)(2,1)} %payload.1), calls=%async_computation.1 | async-start | bytes 4194304 | tf_op jit(solution)/shard_map/all_to_all | solution.py:367
  29.5 2.6 %collective-permute-start.2 = (bf16[80,2048]{1,0:T(8,128)(2,1)}, bf16[80,2048]{1,0:T(8,128)(2,1)}, u32[]{:S(2)}, u32[]{:S(2)}) collective-permute-start(bf16[80,2048]{1,0:T(8,128)(2,1)} %get-tuple-element.15), channel_id=1, source_target_pairs={{0,3},{1,0},{2,1},{3,2},{4,7},{5,4},{6,5},{7,6},{8,11},{9,8},{10,9... | collective-permute-start | bytes 983048 | tf_op jit(solution)/shard_map/ppermute | solution.py:298
  33.3 2.7 %collective-permute-start.8 = (bf16[80,2048]{1,0:T(8,128)(2,1)S(1)}, bf16[80,2048]{1,0:T(8,128)(2,1)S(1)}, u32[]{:S(2)}, u32[]{:S(2)}) collective-permute-start(bf16[80,2048]{1,0:T(8,128)(2,1)S(1)} %get-tuple-element.16), channel_id=1, source_target_pairs={{0,8},{1,9},{2,10},{3,11},{4,12},{5,13},{6,14},{7,15},{8,0},{9,1},... | collective-permute-start | bytes 983048 | tf_op jit(solution)/shard_map/ppermute | solution.py:298
  38.0 20.6 %all-to-all-done.1 = bf16[16,8,64,128]{3,2,1,0:T(8,128)(2,1)S(1)} async-done(((bf16[16,8,64,128]{3,2,1,0:T(8,128)(2,1)}), bf16[16,8,64,128]{3,2,1,0:T(8,128)(2,1)S(1)}, u32[]{:S(2)}, u32[]{:S(2)}) %all-to-all-start.1) | async-done | bytes 2097184 | tf_op jit(solution)/shard_map/all_to_all | solution.py:367
  60.2 7.2 %all-to-all-start.2 = ((bf16[8,16,64,128]{3,2,1,0:T(8,128)(2,1)}), bf16[8,16,64,128]{3,2,1,0:T(8,128)(2,1)S(1)}, u32[]{:S(2)}, u32[]{:S(2)}) async-start(bf16[8,16,64,128]{3,2,1,0:T(8,128)(2,1)} %bitcast.20), calls=%async_computation.2 | async-start | bytes 4194304 | tf_op jit(solution)/shard_map/all_to_all | solution.py:368
  70.7 7.3 %collective-permute-done.9 = bf16[80,2048]{1,0:T(8,128)(2,1)S(1)} collective-permute-done((bf16[80,2048]{1,0:T(8,128)(2,1)S(1)}, bf16[80,2048]{1,0:T(8,128)(2,1)S(1)}, u32[]{:S(2)}, u32[]{:S(2)}) %collective-permute-start.9) | collective-permute-done | bytes 327712 | tf_op jit(solution)/shard_map/ppermute | solution.py:298
  88.4 5.3 %all-to-all-done.2.in_ref = bf16[8,16,64,128]{3,2,1,0:T(8,128)(2,1)S(1)} async-done(((bf16[8,16,64,128]{3,2,1,0:T(8,128)(2,1)}), bf16[8,16,64,128]{3,2,1,0:T(8,128)(2,1)S(1)}, u32[]{:S(2)}, u32[]{:S(2)}) %all-to-all-start.2) | async-done | bytes 2097184 | tf_op jit(solution)/shard_map/all_to_all | solution.py:368
  93.7 16.1 %inverse.1 = (f32[136,128]{1,0:T(8,128)S(1)}, f32[128,128]{1,0:T(8,128)S(1)}, f32[2,256,256]{2,1,0:T(8,128)S(1)}, bf16[16,80,512]{2,1,0:T(8,128)(2,1)S(1)}, bf16[16,80,512]{2,1,0:T(8,128)(2,1)S(1)}) custom-call(s32[32]{0:T(128)S(1)} %pad_add_fusion.rel_ref, f32[3]{0:T(128)S(1)} %add_convert_fusion.lev_ref, bf16[8,16,64,128]{3,2,1,0:T(8,128)(2,1)S(1)} %all-to-all-done.2.in_ref), custom_call_target="tpu_custom_call" | custom-call | tf_op jit(solution)/shard_map/inverse/pallas_call | solution.py:380
  109.9 8.2 %collective-permute-done.21 = f32[128,128]{1,0:T(8,128)S(1)} collective-permute-done((f32[128,128]{1,0:T(8,128)S(1)}, f32[128,128]{1,0:T(8,128)S(1)}, u32[]{:S(2)}, u32[]{:S(2)}) %collective-permute-start.21) | collective-permute-done | bytes 65568 | tf_op jit(solution)/shard_map/ppermute | solution.py:298
  118.1 4.6 %collective-permute-done.22 = f32[128,128]{1,0:T(8,128)S(1)} collective-permute-done((f32[128,128]{1,0:T(8,128)S(1)}, f32[128,128]{1,0:T(8,128)S(1)}, u32[]{:S(2)}, u32[]{:S(2)}) %collective-permute-start.22) | collective-permute-done | bytes 65568 | tf_op jit(solution)/shard_map/ppermute | solution.py:298
  122.7 3.4 %collective-permute-done.23 = f32[128,128]{1,0:T(8,128)S(1)} collective-permute-done((f32[128,128]{1,0:T(8,128)S(1)}, f32[128,128]{1,0:T(8,128)S(1)}, u32[]{:S(2)}, u32[]{:S(2)}) %collective-permute-start.23) | collective-permute-done | bytes 65568 | tf_op jit(solution)/shard_map/ppermute | solution.py:298
  126.1 4.4 %collective-permute-start.14 = (f32[136,128]{1,0:T(8,128)S(1)}, f32[136,128]{1,0:T(8,128)S(1)}, u32[]{:S(2)}, u32[]{:S(2)}) collective-permute-start(f32[136,128]{1,0:T(8,128)S(1)} %get-tuple-element.19), channel_id=1, source_target_pairs={{0,1},{1,2},{2,3},{3,0},{4,5},{5,6},{6,7},{7,4},{8,9},{9,10},{10,1... | collective-permute-start | bytes 208904 | tf_op jit(solution)/shard_map/ppermute | solution.py:298
  130.5 2.3 collective-permute-done.14
  132.8 2.5 %collective-permute-start.15 = (f32[136,128]{1,0:T(8,128)S(1)}, f32[136,128]{1,0:T(8,128)S(1)}, u32[]{:S(2)}, u32[]{:S(2)}) collective-permute-start(f32[136,128]{1,0:T(8,128)S(1)} %get-tuple-element.19), channel_id=1, source_target_pairs={{0,2},{1,3},{2,0},{3,1},{4,6},{5,7},{6,4},{7,5},{8,10},{9,11},{10,... | collective-permute-start | bytes 208904 | tf_op jit(solution)/shard_map/ppermute | solution.py:298
  135.3 2.2 collective-permute-done.15
  145.9 2.0 collective-permute-start.13
  150.8 2.7 %collective-permute-start.6 = (bf16[160,2048]{1,0:T(8,128)(2,1)S(1)}, bf16[160,2048]{1,0:T(8,128)(2,1)S(1)}, u32[]{:S(2)}, u32[]{:S(2)}) collective-permute-start(bf16[160,2048]{1,0:T(8,128)(2,1)S(1)} %slice.41), channel_id=1, source_target_pairs={{0,12},{1,13},{2,14},{3,15},{4,0},{5,1},{6,2},{7,3},{8,4},{9,5},{1... | collective-permute-start | bytes 1966088 | tf_op jit(solution)/shard_map/ppermute | solution.py:298
  153.5 7.8 %collective-permute-done.27 = f32[256,128]{1,0:T(8,128)S(1)} collective-permute-done((f32[256,128]{1,0:T(8,128)S(1)}, f32[256,128]{1,0:T(8,128)S(1)}, u32[]{:S(2)}, u32[]{:S(2)}) %collective-permute-start.27) | collective-permute-done | bytes 131104 | tf_op jit(solution)/shard_map/ppermute | solution.py:298
  162.8 11.9 %collective-permute-done.18 = f32[272,128]{1,0:T(8,128)S(1)} collective-permute-done((f32[272,128]{1,0:T(8,128)S(1)}, f32[272,128]{1,0:T(8,128)S(1)}, u32[]{:S(2)}, u32[]{:S(2)}) %collective-permute-start.18) | collective-permute-done | bytes 139296 | tf_op jit(solution)/shard_map/ppermute | solution.py:298
  174.6 1.9 collective-permute-start.20
  176.6 2.2 collective-permute-done.20
  178.9 20.9 %product.1 = (f32[2048,512]{1,0:T(8,128)S(1)}, f32[2048,512]{1,0:T(8,128)S(1)}, f32[8,128]{1,0:T(8,128)S(1)}) custom-call(s32[32]{0:T(128)S(1)} %pad_add_fusion.rel_ref, bf16[320,2048]{1,0:T(8,128)(2,1)} %constant_dynamic-update-slice_fusion.refs_0_, bf16[320,2048]{1,0:T(8,128)(2,1)} %collective-permute-done.3.refs_1_, ...), custom_call_target="tpu_custom_call" | custom-call | tf_op jit(solution)/shard_map/product/pallas_call | solution.py:406
  199.9 2.0 copy-done.1
  201.9 2.0 copy-done.3
  203.9 17.1 %all_to_all.29 = f32[8,1,128]{2,1,0:T(1,128)S(1)} all-to-all(f32[8,1,128]{2,1,0:T(1,128)S(1)} %broadcast_in_dim.4), channel_id=1, replica_groups=mesh['expert'=8,'shard'=16] {'expert'}, dimensions={0} | all-to-all | bytes 8192 | tf_op jit(solution)/shard_map/all_to_all | solution.py:438
  221.0 12.6 %all_to_all.30 = f32[16,1,128]{2,1,0:T(1,128)S(1)} all-to-all(f32[16,1,128]{2,1,0:T(1,128)S(1)} %broadcast_in_dim.5), channel_id=1, replica_groups=mesh['expert'=8,'shard'=16] {'shard'}, dimensions={0} | all-to-all | bytes 16384 | tf_op jit(solution)/shard_map/all_to_all | solution.py:440
  233.6 2.2 copy-done.2
  235.8 2.2 copy-done.4
  238.0 2.9 %scale.1 = bf16[2,2048,512]{2,1,0:T(8,128)(2,1)} custom-call(f32[16,128]{1,0:T(8,128)S(1)} %bitcast.19, f32[2048,512]{1,0:T(8,128)S(1)} %copy-done.2, f32[2048,512]{1,0:T(8,128)S(1)} %copy-done.4), custom_call_target="tpu_custom_call" | custom-call | tf_op jit(solution)/shard_map/scale/pallas_call | solution.py:442
  (102 shorter events, 37.4 us)
Async XLA Ops:
  0.0 86.7 %copy-start = (s32[1,16]{1,0:T(1,128)S(1)}, s32[1,16]{1,0:T(1,128)}, u32[]{:S(2)}) copy-start(s32[1,16]{1,0:T(1,128)} %param.8) | copy-start | bytes 196
  3.9 16.7 %all-to-all-start = ((bf16[8,40,1024]{2,1,0:T(8,128)(2,1)}), bf16[8,40,1024]{2,1,0:T(8,128)(2,1)S(1)}, u32[]{:S(2)}, u32[]{:S(2)}) async-start(bf16[8,40,1024]{2,1,0:T(8,128)(2,1)} %bitcast.2), calls=%async_computation | async-start | bytes 1310720 | tf_op jit(solution)/shard_map/all_to_all | solution.py:338
  20.6 38.0 %all-to-all-start.1 = ((bf16[16,8,64,128]{3,2,1,0:T(8,128)(2,1)}), bf16[16,8,64,128]{3,2,1,0:T(8,128)(2,1)S(1)}, u32[]{:S(2)}, u32[]{:S(2)}) async-start(bf16[16,8,64,128]{3,2,1,0:T(8,128)(2,1)} %payload.1), calls=%async_computation.1 | async-start | bytes 4194304 | tf_op jit(solution)/shard_map/all_to_all | solution.py:367
  29.5 54.2 %collective-permute-start.2 = (bf16[80,2048]{1,0:T(8,128)(2,1)}, bf16[80,2048]{1,0:T(8,128)(2,1)}, u32[]{:S(2)}, u32[]{:S(2)}) collective-permute-start(bf16[80,2048]{1,0:T(8,128)(2,1)} %get-tuple-element.15), channel_id=1, source_target_pairs={{0,3},{1,0},{2,1},{3,2},{4,7},{5,4},{6,5},{7,6},{8,11},{9,8},{10,9... | collective-permute-start | bytes 983048 | tf_op jit(solution)/shard_map/ppermute | solution.py:298
  32.1 49.9 %collective-permute-start.1 = (bf16[80,2048]{1,0:T(8,128)(2,1)}, bf16[80,2048]{1,0:T(8,128)(2,1)}, u32[]{:S(2)}, u32[]{:S(2)}) collective-permute-start(bf16[80,2048]{1,0:T(8,128)(2,1)} %get-tuple-element.15), channel_id=1, source_target_pairs={{0,2},{1,3},{2,0},{3,1},{4,6},{5,7},{6,4},{7,5},{8,10},{9,11},{10,... | collective-permute-start | bytes 983048 | tf_op jit(solution)/shard_map/ppermute | solution.py:298
  32.7 47.6 %collective-permute-start = (bf16[80,2048]{1,0:T(8,128)(2,1)}, bf16[80,2048]{1,0:T(8,128)(2,1)}, u32[]{:S(2)}, u32[]{:S(2)}) collective-permute-start(bf16[80,2048]{1,0:T(8,128)(2,1)} %get-tuple-element.15), channel_id=1, source_target_pairs={{0,1},{1,2},{2,3},{3,0},{4,5},{5,6},{6,7},{7,4},{8,9},{9,10},{10,1... | collective-permute-start | bytes 983048 | tf_op jit(solution)/shard_map/ppermute | solution.py:298
  33.3 36.7 %collective-permute-start.8 = (bf16[80,2048]{1,0:T(8,128)(2,1)S(1)}, bf16[80,2048]{1,0:T(8,128)(2,1)S(1)}, u32[]{:S(2)}, u32[]{:S(2)}) collective-permute-start(bf16[80,2048]{1,0:T(8,128)(2,1)S(1)} %get-tuple-element.16), channel_id=1, source_target_pairs={{0,8},{1,9},{2,10},{3,11},{4,12},{5,13},{6,14},{7,15},{8,0},{9,1},... | collective-permute-start | bytes 983048 | tf_op jit(solution)/shard_map/ppermute | solution.py:298
  36.0 33.2 %collective-permute-start.7 = (bf16[80,2048]{1,0:T(8,128)(2,1)S(1)}, bf16[80,2048]{1,0:T(8,128)(2,1)S(1)}, u32[]{:S(2)}, u32[]{:S(2)}) collective-permute-start(bf16[80,2048]{1,0:T(8,128)(2,1)S(1)} %get-tuple-element.16), channel_id=1, source_target_pairs={{0,4},{1,5},{2,6},{3,7},{4,8},{5,9},{6,10},{7,11},{8,12},{9,13},{1... | collective-permute-start | bytes 983048 | tf_op jit(solution)/shard_map/ppermute | solution.py:298
  60.2 33.5 %all-to-all-start.2 = ((bf16[8,16,64,128]{3,2,1,0:T(8,128)(2,1)}), bf16[8,16,64,128]{3,2,1,0:T(8,128)(2,1)S(1)}, u32[]{:S(2)}, u32[]{:S(2)}) async-start(bf16[8,16,64,128]{3,2,1,0:T(8,128)(2,1)} %bitcast.20), calls=%async_computation.2 | async-start | bytes 4194304 | tf_op jit(solution)/shard_map/all_to_all | solution.py:368
  69.1 8.9 %collective-permute-start.9 = (bf16[80,2048]{1,0:T(8,128)(2,1)S(1)}, bf16[80,2048]{1,0:T(8,128)(2,1)S(1)}, u32[]{:S(2)}, u32[]{:S(2)}) collective-permute-start(bf16[80,2048]{1,0:T(8,128)(2,1)S(1)} %get-tuple-element.16), channel_id=1, source_target_pairs={{0,12},{1,13},{2,14},{3,15},{4,0},{5,1},{6,2},{7,3},{8,4},{9,5},{1... | collective-permute-start | bytes 983048 | tf_op jit(solution)/shard_map/ppermute | solution.py:298
  78.8 60.4 %collective-permute-start.12 = (bf16[320,2048]{1,0:T(8,128)(2,1)}, bf16[320,2048]{1,0:T(8,128)(2,1)S(1)}, u32[]{:S(2)}, u32[]{:S(2)}) collective-permute-start(bf16[320,2048]{1,0:T(8,128)(2,1)} %constant_dynamic-update-slice_fusion.4.refs_5_), channel_id=1, source_target_pairs={{0,3},{1,0},{2,1},{3,2},{4,7},{5,4},{6,5},{7,6},{8,11},{9,8},{10,9... | collective-permute-start | bytes 3932168 | tf_op jit(solution)/shard_map/ppermute | solution.py:298
  79.9 62.1 %collective-permute-start.10 = (bf16[320,2048]{1,0:T(8,128)(2,1)}, bf16[320,2048]{1,0:T(8,128)(2,1)}, u32[]{:S(2)}, u32[]{:S(2)}) collective-permute-start(bf16[320,2048]{1,0:T(8,128)(2,1)} %constant_dynamic-update-slice_fusion.4.refs_5_), channel_id=1, source_target_pairs={{0,1},{1,2},{2,3},{3,0},{4,5},{5,6},{6,7},{7,4},{8,9},{9,10},{10,1... | collective-permute-start | bytes 3932168 | tf_op jit(solution)/shard_map/ppermute | solution.py:298
  85.5 58.0 %collective-permute-start.5 = (bf16[320,2048]{1,0:T(8,128)(2,1)}, bf16[320,2048]{1,0:T(8,128)(2,1)}, u32[]{:S(2)}, u32[]{:S(2)}) collective-permute-start(bf16[320,2048]{1,0:T(8,128)(2,1)} %constant_dynamic-update-slice_fusion.refs_0_), channel_id=1, source_target_pairs={{0,12},{1,13},{2,14},{3,15},{4,0},{5,1},{6,2},{7,3},{8,4},{9,5},{1... | collective-permute-start | bytes 3932168 | tf_op jit(solution)/shard_map/ppermute | solution.py:298
  87.3 58.5 %collective-permute-start.3 = (bf16[320,2048]{1,0:T(8,128)(2,1)}, bf16[320,2048]{1,0:T(8,128)(2,1)}, u32[]{:S(2)}, u32[]{:S(2)}) collective-permute-start(bf16[320,2048]{1,0:T(8,128)(2,1)} %constant_dynamic-update-slice_fusion.refs_0_), channel_id=1, source_target_pairs={{0,4},{1,5},{2,6},{3,7},{4,8},{5,9},{6,10},{7,11},{8,12},{9,13},{1... | collective-permute-start | bytes 3932168 | tf_op jit(solution)/shard_map/ppermute | solution.py:298
  109.8 8.3 %collective-permute-start.21 = (f32[128,128]{1,0:T(8,128)S(1)}, f32[128,128]{1,0:T(8,128)S(1)}, u32[]{:S(2)}, u32[]{:S(2)}) collective-permute-start(f32[128,128]{1,0:T(8,128)S(1)} %get-tuple-element.20), channel_id=1, source_target_pairs={{0,4},{1,5},{2,6},{3,7},{4,8},{5,9},{6,10},{7,11},{8,12},{9,13},{1... | collective-permute-start | bytes 196616 | tf_op jit(solution)/shard_map/ppermute | solution.py:298
  118.1 4.6 %collective-permute-start.22 = (f32[128,128]{1,0:T(8,128)S(1)}, f32[128,128]{1,0:T(8,128)S(1)}, u32[]{:S(2)}, u32[]{:S(2)}) collective-permute-start(f32[128,128]{1,0:T(8,128)S(1)} %get-tuple-element.20), channel_id=1, source_target_pairs={{0,8},{1,9},{2,10},{3,11},{4,12},{5,13},{6,14},{7,15},{8,0},{9,1},... | collective-permute-start | bytes 196616 | tf_op jit(solution)/shard_map/ppermute | solution.py:298
  122.7 3.4 %collective-permute-start.23 = (f32[128,128]{1,0:T(8,128)S(1)}, f32[128,128]{1,0:T(8,128)S(1)}, u32[]{:S(2)}, u32[]{:S(2)}) collective-permute-start(f32[128,128]{1,0:T(8,128)S(1)} %get-tuple-element.20), channel_id=1, source_target_pairs={{0,12},{1,13},{2,14},{3,15},{4,0},{5,1},{6,2},{7,3},{8,4},{9,5},{1... | collective-permute-start | bytes 196616 | tf_op jit(solution)/shard_map/ppermute | solution.py:298
  126.1 6.7 %collective-permute-start.14 = (f32[136,128]{1,0:T(8,128)S(1)}, f32[136,128]{1,0:T(8,128)S(1)}, u32[]{:S(2)}, u32[]{:S(2)}) collective-permute-start(f32[136,128]{1,0:T(8,128)S(1)} %get-tuple-element.19), channel_id=1, source_target_pairs={{0,1},{1,2},{2,3},{3,0},{4,5},{5,6},{6,7},{7,4},{8,9},{9,10},{10,1... | collective-permute-start | bytes 208904 | tf_op jit(solution)/shard_map/ppermute | solution.py:298
  132.8 4.7 %collective-permute-start.15 = (f32[136,128]{1,0:T(8,128)S(1)}, f32[136,128]{1,0:T(8,128)S(1)}, u32[]{:S(2)}, u32[]{:S(2)}) collective-permute-start(f32[136,128]{1,0:T(8,128)S(1)} %get-tuple-element.19), channel_id=1, source_target_pairs={{0,2},{1,3},{2,0},{3,1},{4,6},{5,7},{6,4},{7,5},{8,10},{9,11},{10,... | collective-permute-start | bytes 208904 | tf_op jit(solution)/shard_map/ppermute | solution.py:298
  137.5 3.6 %collective-permute-start.16 = (f32[136,128]{1,0:T(8,128)S(1)}, f32[136,128]{1,0:T(8,128)S(1)}, u32[]{:S(2)}, u32[]{:S(2)}) collective-permute-start(f32[136,128]{1,0:T(8,128)S(1)} %get-tuple-element.19), channel_id=1, source_target_pairs={{0,3},{1,0},{2,1},{3,2},{4,7},{5,4},{6,5},{7,6},{8,11},{9,8},{10,9... | collective-permute-start | bytes 208904 | tf_op jit(solution)/shard_map/ppermute | solution.py:298
  139.3 9.7 %collective-permute-start.26 = (f32[512,128]{1,0:T(8,128)S(1)}, f32[512,128]{1,0:T(8,128)S(1)}, u32[]{:S(2)}, u32[]{:S(2)}) collective-permute-start(f32[512,128]{1,0:T(8,128)S(1)} %get-tuple-element.33), channel_id=1, source_target_pairs={{0,3},{1,0},{2,1},{3,2},{4,7},{5,4},{6,5},{7,6},{8,11},{9,8},{10,9... | collective-permute-start | bytes 786440 | tf_op jit(solution)/shard_map/ppermute | solution.py:298
  141.2 9.1 %collective-permute-start.24 = (f32[512,128]{1,0:T(8,128)S(1)}, f32[512,128]{1,0:T(8,128)S(1)}, u32[]{:S(2)}, u32[]{:S(2)}) collective-permute-start(f32[512,128]{1,0:T(8,128)S(1)} %get-tuple-element.33), channel_id=1, source_target_pairs={{0,1},{1,2},{2,3},{3,0},{4,5},{5,6},{6,7},{7,4},{8,9},{9,10},{10,1... | collective-permute-start | bytes 786440 | tf_op jit(solution)/shard_map/ppermute | solution.py:298
  142.0 8.7 %collective-permute-start.19 = (f32[544,128]{1,0:T(8,128)S(1)}, f32[544,128]{1,0:T(8,128)S(1)}, u32[]{:S(2)}, u32[]{:S(2)}) collective-permute-start(f32[544,128]{1,0:T(8,128)S(1)} %get-tuple-element.25), channel_id=1, source_target_pairs={{0,12},{1,13},{2,14},{3,15},{4,0},{5,1},{6,2},{7,3},{8,4},{9,5},{1... | collective-permute-start | bytes 835592 | tf_op jit(solution)/shard_map/ppermute | solution.py:298
  143.4 7.3 %collective-permute-start.17 = (f32[544,128]{1,0:T(8,128)S(1)}, f32[544,128]{1,0:T(8,128)S(1)}, u32[]{:S(2)}, u32[]{:S(2)}) collective-permute-start(f32[544,128]{1,0:T(8,128)S(1)} %get-tuple-element.25), channel_id=1, source_target_pairs={{0,4},{1,5},{2,6},{3,7},{4,8},{5,9},{6,10},{7,11},{8,12},{9,13},{1... | collective-permute-start | bytes 835592 | tf_op jit(solution)/shard_map/ppermute | solution.py:298
  145.9 33.0 %collective-permute-start.13 = (bf16[160,2048]{1,0:T(8,128)(2,1)S(1)}, bf16[160,2048]{1,0:T(8,128)(2,1)S(1)}, u32[]{:S(2)}, u32[]{:S(2)}) collective-permute-start(bf16[160,2048]{1,0:T(8,128)(2,1)S(1)} %slice.43), channel_id=1, source_target_pairs={{0,3},{1,0},{2,1},{3,2},{4,7},{5,4},{6,5},{7,6},{8,11},{9,8},{10,9... | collective-permute-start | bytes 1966088 | tf_op jit(solution)/shard_map/ppermute | solution.py:298
  149.0 12.3 %collective-permute-start.27 = (f32[256,128]{1,0:T(8,128)S(1)}, f32[256,128]{1,0:T(8,128)S(1)}, u32[]{:S(2)}, u32[]{:S(2)}) collective-permute-start(f32[256,128]{1,0:T(8,128)S(1)} %slice.47), channel_id=1, source_target_pairs={{0,3},{1,0},{2,1},{3,2},{4,7},{5,4},{6,5},{7,6},{8,11},{9,8},{10,9... | collective-permute-start | bytes 393224 | tf_op jit(solution)/shard_map/ppermute | solution.py:298
  150.3 11.3 %collective-permute-start.25 = (f32[256,128]{1,0:T(8,128)S(1)}, f32[256,128]{1,0:T(8,128)S(1)}, u32[]{:S(2)}, u32[]{:S(2)}) collective-permute-start(f32[256,128]{1,0:T(8,128)S(1)} %slice.46), channel_id=1, source_target_pairs={{0,1},{1,2},{2,3},{3,0},{4,5},{5,6},{6,7},{7,4},{8,9},{9,10},{10,1... | collective-permute-start | bytes 393224 | tf_op jit(solution)/shard_map/ppermute | solution.py:298
  150.7 28.2 %collective-permute-start.11 = (bf16[160,2048]{1,0:T(8,128)(2,1)S(1)}, bf16[160,2048]{1,0:T(8,128)(2,1)S(1)}, u32[]{:S(2)}, u32[]{:S(2)}) collective-permute-start(bf16[160,2048]{1,0:T(8,128)(2,1)S(1)} %slice.42), channel_id=1, source_target_pairs={{0,1},{1,2},{2,3},{3,0},{4,5},{5,6},{6,7},{7,4},{8,9},{9,10},{10,1... | collective-permute-start | bytes 1966088 | tf_op jit(solution)/shard_map/ppermute | solution.py:298
  150.8 28.1 %collective-permute-start.6 = (bf16[160,2048]{1,0:T(8,128)(2,1)S(1)}, bf16[160,2048]{1,0:T(8,128)(2,1)S(1)}, u32[]{:S(2)}, u32[]{:S(2)}) collective-permute-start(bf16[160,2048]{1,0:T(8,128)(2,1)S(1)} %slice.41), channel_id=1, source_target_pairs={{0,12},{1,13},{2,14},{3,15},{4,0},{5,1},{6,2},{7,3},{8,4},{9,5},{1... | collective-permute-start | bytes 1966088 | tf_op jit(solution)/shard_map/ppermute | solution.py:298
  161.3 17.6 %collective-permute-start.4 = (bf16[160,2048]{1,0:T(8,128)(2,1)S(1)}, bf16[160,2048]{1,0:T(8,128)(2,1)S(1)}, u32[]{:S(2)}, u32[]{:S(2)}) collective-permute-start(bf16[160,2048]{1,0:T(8,128)(2,1)S(1)} %slice.40), channel_id=1, source_target_pairs={{0,4},{1,5},{2,6},{3,7},{4,8},{5,9},{6,10},{7,11},{8,12},{9,13},{1... | collective-permute-start | bytes 1966088 | tf_op jit(solution)/shard_map/ppermute | solution.py:298
  161.6 13.0 %collective-permute-start.18 = (f32[272,128]{1,0:T(8,128)S(1)}, f32[272,128]{1,0:T(8,128)S(1)}, u32[]{:S(2)}, u32[]{:S(2)}) collective-permute-start(f32[272,128]{1,0:T(8,128)S(1)} %slice.44), channel_id=1, source_target_pairs={{0,4},{1,5},{2,6},{3,7},{4,8},{5,9},{6,10},{7,11},{8,12},{9,13},{1... | collective-permute-start | bytes 417800 | tf_op jit(solution)/shard_map/ppermute | solution.py:298
  174.6 4.2 %collective-permute-start.20 = (f32[272,128]{1,0:T(8,128)S(1)}, f32[272,128]{1,0:T(8,128)S(1)}, u32[]{:S(2)}, u32[]{:S(2)}) collective-permute-start(f32[272,128]{1,0:T(8,128)S(1)} %slice.45), channel_id=1, source_target_pairs={{0,12},{1,13},{2,14},{3,15},{4,0},{5,1},{6,2},{7,3},{8,4},{9,5},{1... | collective-permute-start | bytes 417800 | tf_op jit(solution)/shard_map/ppermute | solution.py:298
  (8 other events, 34.3 us)
